TPU v7x, 32 devices: a whole 2x2x4 slice. The times are simulated.
32 devices in a mesh: rep: 4 (over x, core), dom: 8 (over z, y).
Axes of the slice: x: 2, y: 2, z: 4, core: 2. Of those that a mesh axis runs over, the one named last changes fastest.
Arguments:
- coords: float32 [4, 3, 32768], P('rep', None, 'dom'), may hold values from -6 to 6
- atom_var: float32 [32768], P('dom'), may hold values from 0.2 to 1
- atom_weight: float32 [32768], P('dom'), may hold values from 0.5 to 2
- atoms_live: int32 [256], P('dom'), may hold values from 1 to 128, 24576 in all
- block_list: int32 [256, 16], P('dom'), may hold values from 0 to 2047, as said below
- owner_map: int32 [2048], replicated, may hold values from 0 to 2047, as said below
- comp_means: float32 [3, 262144], replicated, may hold values from -6 to 6
- comp_var: float32 [262144], replicated, may hold values from 0.3 to 1.5
- comp_weight: float32 [262144], replicated, may hold values from 0.1 to 1
- target: float32 [262144], P('dom'), may hold values from 0 to 2
- noise_sigma: float32 [262144], P('dom'), may hold values from 0.05 to 0.5
Outputs:
- intersection_avg: float32 [262144], P('dom')
- forces: float32 [4, 3, 32768], P('rep', None, 'dom')
Inputs may be any that keep to these rules, and one draw needn't show every extreme that they name: `atoms_live`: entry a is the number of live atoms of atom block a, held in the first slots of the block. `owner_map`: A permutation of the component blocks. Storage position p lies on dom index p // 256. `block_list`: of the 32 x 16 entries of one dom index's atom blocks, at most 64 name blocks whose storage position lies on any one dom index, and in every draw some dom index receives exactly 64 entries from every dom index. An atom block may list a component block more than once; each entry counts.
All inputs are finite; a program needn't handle non-finite values.
Results may differ from a plain program's by a relative error of at most 0.0003.
Values sent between devices are 32-bit elements; how exact they have to be, the bound alone decides.
A program may use at most 128 MiB of HBM per device.

v0:
```python
import functools
import math

import jax
import jax.numpy as jnp
from jax import lax
from jax.experimental import pallas as pl
from jax.experimental.pallas import tpu as pltpu
from jax.sharding import PartitionSpec as P

CAPACITY = 64
ROWS = CAPACITY + 8
LANES = 128
SUB = 32
HALF = 16
OUT_SLOTS = 3
IN_SLOTS = 5

energy_unit = 2.494
norm = (2.0 * math.pi) ** -1.5
half_log2e = -0.5 / math.log(2.0)
VMEM = pltpu.VMEM
MESH = pl.DeviceIdType.MESH


def three(value):
    first = value.astype(jnp.bfloat16)
    rest = value - first.astype(jnp.float32)
    second = rest.astype(jnp.bfloat16)
    third = (rest - second.astype(jnp.float32)).astype(jnp.bfloat16)
    return first, second, third


def three_f32(value):
    return [piece.astype(jnp.float32) for piece in three(value)]


def pair_kernel(
    listed, owned, live_h, lst_h, owner_h, x_h, av_h, aw_h, m_h, cv_h, cw_h,
    send_ref, pos_ref, table_ref, g_h,
    g_buf, g_sems, live, lst, owner, x_v, av_v, aw_v, m_v, cv_v, cw_v, count, avb, wb, sems,
):
    domains = send_ref.shape[0]
    blocks = live.shape[0]
    loads = [
        pltpu.make_async_copy(src, dst, sems.at[i])
        for i, (src, dst) in enumerate(
            [(m_h, m_v), (cv_h, cv_v), (cw_h, cw_v), (x_h, x_v), (av_h, av_v), (aw_h, aw_v),
             (owner_h, owner), (lst_h, lst), (live_h, live)]
        )
    ]
    for load in loads:
        load.start()
    send_ref[...] = jnp.zeros_like(send_ref)
    send_ref[:, CAPACITY : CAPACITY + 8, :] = jnp.full((domains, 8, LANES), -1.0, jnp.float32)
    for d in range(domains):
        count[d] = 0
    for load in loads:
        load.wait()
    lane = lax.broadcasted_iota(jnp.int32, (1, LANES), 1)
    one = jnp.ones((1, LANES), jnp.float32)
    none = jnp.zeros((3, LANES), jnp.float32)

    def out_copy(a):
        turn = lax.rem(a, OUT_SLOTS)
        return pltpu.make_async_copy(g_buf.at[turn], g_h.at[a], g_sems.at[turn])

    def block(a, carry):
        turn = lax.rem(a, OUT_SLOTS)

        @pl.when(a >= OUT_SLOTS)
        def _():
            out_copy(a - OUT_SLOTS).wait()

        x = jnp.concatenate(
            [x_v[c, :, pl.ds(pl.multiple_of(a * LANES, LANES), LANES)] for c in range(3)], axis=0
        )
        weights = jnp.where(lane < live[a], aw_v[pl.ds(a, 1), :], 0.0)
        avb[...] = jnp.transpose(jnp.broadcast_to(av_v[pl.ds(a, 1), :], (LANES, LANES)))
        wb[...] = jnp.transpose(jnp.broadcast_to(weights, (LANES, LANES)))
        xx = jnp.sum(x * x, axis=0, keepdims=True)
        left = half_log2e * jnp.concatenate([-2.0 * x, one, xx, none], axis=0)
        l0, l1, l2 = three_f32(left)
        lhs = jnp.concatenate([l0, l0, l1, l1, l0, l2], axis=0).astype(jnp.bfloat16)
        for k in range(listed):
            e = a * listed + k
            b = lst[e]
            m = m_v[:, pl.ds(pl.multiple_of(b * LANES, LANES), LANES)]
            mm = jnp.sum(m * m, axis=0, keepdims=True)
            r0, r1, r2 = three_f32(jnp.concatenate([m, mm, one, none], axis=0))
            rhs = jnp.concatenate([r0, r1, r0, r1, r2, r0], axis=0).astype(jnp.bfloat16)
            scaled = lax.dot_general(
                lhs, rhs, (((0,), (0,)), ((), ())), preferred_element_type=jnp.float32
            )
            cv = cv_v[pl.ds(b, 1), :]
            total = jnp.zeros((SUB, LANES), jnp.float32)
            for h in range(LANES // SUB):
                rows = slice(h * SUB, (h + 1) * SUB)
                root = lax.rsqrt(avb[rows, :] + cv)
                inv = root * root
                ov = (root * inv) * jnp.exp2(scaled[rows] * inv) * wb[rows, :]
                g_buf[turn, k * LANES + h * SUB : k * LANES + (h + 1) * SUB, :] = ov * inv
                total = total + ov
            scale = norm * cw_v[pl.ds(b, 1), :]
            table_ref[e] = scale * jnp.concatenate([one, m], axis=0)
            partial = jnp.sum(total, axis=0, keepdims=True) * scale
            place = owner[b]
            dev = lax.div(place, owned)
            slot = place - dev * owned
            rank = count[dev]
            count[dev] = rank + 1
            pos_ref[e] = dev * CAPACITY + rank
            send_ref[dev, pl.ds(rank, 1), :] = partial
            before = send_ref[dev, CAPACITY : CAPACITY + 1, :]
            send_ref[dev, CAPACITY : CAPACITY + 1, :] = jnp.where(
                lane == rank, slot.astype(jnp.float32), before
            )
        out_copy(a).start()
        return carry

    lax.fori_loop(0, blocks, block, 0)
    for last in range(max(0, blocks - OUT_SLOTS), blocks):
        out_copy(last).wait()


def force_kernel(
    listed, pos_h, x_h, g_h, ret_ref, table_ref, mean_v, f_ref, mean_h,
    g_buf, g_sems, pos, x_v, coef, sums, sems,
):
    blocks = x_v.shape[2] // LANES
    loads = [
        pltpu.make_async_copy(src, dst, sems.at[i])
        for i, (src, dst) in enumerate([(pos_h, pos), (x_h, x_v), (mean_v, mean_h)])
    ]
    for load in loads:
        load.start()
    for load in loads[:2]:
        load.wait()
    ones = jnp.ones((8, LANES), jnp.float32)

    def in_copy(a):
        turn = lax.rem(a, IN_SLOTS)
        return pltpu.make_async_copy(g_h.at[a], g_buf.at[turn], g_sems.at[turn])

    for first in range(min(IN_SLOTS - 1, blocks)):
        in_copy(first).start()

    def block(a, carry):
        turn = lax.rem(a, IN_SLOTS)

        @pl.when(a + IN_SLOTS - 1 < blocks)
        def _():
            in_copy(a + IN_SLOTS - 1).start()

        in_copy(a).wait()
        for k in range(listed):
            e = a * listed + k
            scale = energy_unit * ret_ref[pl.ds(pos[e], 1), :]
            rows = table_ref[e] * scale
            for c in range(4):
                coef[k, c] = jnp.broadcast_to(rows[c : c + 1], (8, LANES))
        for h in range(LANES // HALF):
            acc = [[jnp.zeros((8, LANES), jnp.float32) for _ in range(HALF // 8)] for _ in range(4)]
            for k in range(listed):
                for q in range(HALF // 8):
                    start = k * LANES + h * HALF + q * 8
                    g = g_buf[turn, start : start + 8, :]
                    for c in range(4):
                        acc[c][q] = acc[c][q] + g * coef[k, c]
            for c in range(4):
                for q in range(HALF // 8):
                    sums[c, h * HALF + q * 8 : h * HALF + q * 8 + 8, :] = acc[c][q]
        flat = [
            lax.dot_general(
                ones, sums[c], (((1,), (1,)), ((), ())), precision=lax.Precision.HIGHEST,
                preferred_element_type=jnp.float32,
            )[0:1]
            for c in range(4)
        ]
        here = pl.ds(pl.multiple_of(a * LANES, LANES), LANES)
        for c in range(3):
            f_ref[c, :, here] = x_v[c, :, here] * flat[0] - flat[c + 1]
        return carry

    lax.fori_loop(0, blocks, block, 0)
    loads[2].wait()


def exchange_kernel(
    domains, replicas, send_ref, target_h, sigma_h, mean_ref, ret_ref,
    target_ref, sigma_ref, loads, got, acc, part, back, land, out_send, out_recv, rep_send, rep_recv, back_send, back_recv,
):
    me_d = lax.axis_index("dom")
    me_r = lax.axis_index("rep")
    owned = target_ref.shape[0]
    stages = replicas.bit_length() - 1
    partners = []
    for t in range(stages):
        bit = 1 << t
        partners.append(me_r + bit - 2 * bit * lax.rem(lax.div(me_r, bit), 2))
    fetches = [
        pltpu.make_async_copy(target_h, target_ref, loads.at[0]),
        pltpu.make_async_copy(sigma_h, sigma_ref, loads.at[1]),
    ]
    for fetch in fetches:
        fetch.start()
    barrier = pltpu.get_barrier_semaphore()
    for s in range(1, domains):
        pl.semaphore_signal(
            barrier, inc=1, device_id=(me_r, lax.rem(me_d + s, domains)), device_id_type=MESH
        )
    for t in range(stages):
        pl.semaphore_signal(barrier, inc=1, device_id=(partners[t], me_d), device_id_type=MESH)
    pl.semaphore_wait(barrier, domains - 1 + stages)

    outs = [None]
    for s in range(1, domains):
        peer = lax.rem(me_d + s, domains)
        copy = pltpu.make_async_remote_copy(
            src_ref=send_ref.at[peer],
            dst_ref=got.at[s],
            send_sem=out_send.at[s],
            recv_sem=out_recv.at[s],
            device_id=(me_r, peer),
            device_id_type=MESH,
        )
        copy.start()
        outs.append(copy)

    row = lax.broadcasted_iota(jnp.int32, (owned, CAPACITY), 0).astype(jnp.float32)

    def picks_of(s):
        slots = (
            send_ref[me_d, CAPACITY : CAPACITY + 1, :] if s == 0 else got[s, CAPACITY : CAPACITY + 1, :]
        )
        return jnp.where(row == slots[:, :CAPACITY], 1.0, 0.0).astype(jnp.bfloat16)

    total = jnp.zeros((owned, LANES), jnp.float32)
    for s in range(domains):
        if s:
            outs[s].wait_recv()
        rows = send_ref[me_d, :CAPACITY, :] if s == 0 else got[s, :CAPACITY, :]
        picks = picks_of(s)
        for piece in three(rows):
            total = total + jnp.dot(picks, piece, preferred_element_type=jnp.float32)
    acc[0] = total
    swaps = []
    for t in range(stages):
        copy = pltpu.make_async_remote_copy(
            src_ref=acc.at[t],
            dst_ref=part.at[t],
            send_sem=rep_send.at[t],
            recv_sem=rep_recv.at[t],
            device_id=(partners[t], me_d),
            device_id_type=MESH,
        )
        copy.start()
        swaps.append(copy)
        copy.wait_recv()
        total = total + part[t]
        if t + 1 < stages:
            acc[t + 1] = total
    mean = total / replicas
    mean_ref[...] = mean
    for fetch in fetches:
        fetch.wait()
    misfit = mean - target_ref[...]
    sigmas = sigma_ref[...]
    adjoint = misfit / (sigmas * sigmas + 0.5 * misfit * misfit) / replicas
    pieces = three(adjoint)
    backs = []
    for s in list(range(1, domains)) + [0]:
        picks = picks_of(s)
        rows = jnp.zeros((CAPACITY, LANES), jnp.float32)
        for piece in pieces:
            rows = rows + lax.dot_general(
                picks, piece, (((0,), (0,)), ((), ())), preferred_element_type=jnp.float32
            )
        if s == 0:
            ret_ref[me_d] = rows
            continue
        back[s] = rows
        peer = lax.rem(me_d + domains - s, domains)
        copy = pltpu.make_async_remote_copy(
            src_ref=back.at[s],
            dst_ref=land.at[s],
            send_sem=back_send.at[s],
            recv_sem=back_recv.at[s],
            device_id=(me_r, peer),
            device_id_type=MESH,
        )
        copy.start()
        backs.append((s, copy))
    for s, copy in backs:
        copy.wait_recv()
        ret_ref[lax.rem(me_d + s, domains)] = land[s]
    for copy in outs[1:] + swaps + [copy for _, copy in backs]:
        copy.wait_send()


def shards(
    coords, atom_var, atom_weight, atoms_live, block_list, owner_map,
    comp_means, comp_var, comp_weight, target, noise_sigma,
):
    replicas = lax.axis_size("rep")
    domains = lax.axis_size("dom")
    blocks, listed = block_list.shape
    comp_blocks = owner_map.shape[0]
    owned = target.shape[0] // LANES
    entries = blocks * listed
    x = coords.transpose(1, 0, 2)
    lst = block_list.reshape(-1)
    cv = comp_var.reshape(comp_blocks, LANES)
    cw = comp_weight.reshape(comp_blocks, LANES)
    f32, i32 = jnp.float32, jnp.int32
    whole = pl.BlockSpec(memory_space=VMEM)
    far = pl.BlockSpec(memory_space=pltpu.HBM)
    send, pos, table, g = pl.pallas_call(
        functools.partial(pair_kernel, listed, owned),
        in_specs=[far] * 9,
        out_specs=[whole, pl.BlockSpec(memory_space=pltpu.SMEM), whole, far],
        out_shape=[
            jax.ShapeDtypeStruct((domains, ROWS, LANES), f32),
            jax.ShapeDtypeStruct((entries,), i32),
            jax.ShapeDtypeStruct((entries, 4, LANES), f32),
            jax.ShapeDtypeStruct((blocks, listed * LANES, LANES), f32),
        ],
        scratch_shapes=[
            VMEM((OUT_SLOTS, listed * LANES, LANES), f32),
            pltpu.SemaphoreType.DMA((OUT_SLOTS,)),
            pltpu.SMEM((blocks,), i32),
            pltpu.SMEM((entries,), i32),
            pltpu.SMEM((comp_blocks,), i32),
            VMEM(x.shape, f32),
            VMEM((blocks, LANES), f32),
            VMEM((blocks, LANES), f32),
            VMEM(comp_means.shape, f32),
            VMEM(cv.shape, f32),
            VMEM(cw.shape, f32),
            pltpu.SMEM((domains,), i32),
            VMEM((LANES, LANES), f32),
            VMEM((LANES, LANES), f32),
            pltpu.SemaphoreType.DMA((9,)),
        ],
        compiler_params=pltpu.CompilerParams(vmem_limit_bytes=57 << 20),
        name="pairs",
    )(
        atoms_live, lst, owner_map, x,
        atom_var.reshape(blocks, LANES), atom_weight.reshape(blocks, LANES),
        comp_means, cv, cw,
    )
    stages = replicas.bit_length() - 1
    mean, ret = pl.pallas_call(
        functools.partial(exchange_kernel, domains, replicas),
        in_specs=[whole, far, far],
        out_specs=[whole] * 2,
        out_shape=[
            jax.ShapeDtypeStruct((owned, LANES), f32),
            jax.ShapeDtypeStruct((domains, CAPACITY, LANES), f32),
        ],
        scratch_shapes=[
            VMEM((owned, LANES), f32),
            VMEM((owned, LANES), f32),
            pltpu.SemaphoreType.DMA((2,)),
            VMEM((domains, ROWS, LANES), f32),
            VMEM((stages, owned, LANES), f32),
            VMEM((stages, owned, LANES), f32),
            VMEM((domains, CAPACITY, LANES), f32),
            VMEM((domains, CAPACITY, LANES), f32),
            pltpu.SemaphoreType.DMA((domains,)),
            pltpu.SemaphoreType.DMA((domains,)),
            pltpu.SemaphoreType.DMA((stages,)),
            pltpu.SemaphoreType.DMA((stages,)),
            pltpu.SemaphoreType.DMA((domains,)),
            pltpu.SemaphoreType.DMA((domains,)),
        ],
        compiler_params=pltpu.CompilerParams(
            collective_id=0, has_side_effects=True, vmem_limit_bytes=57 << 20
        ),
        name="exchange",
    )(send, target.reshape(owned, LANES), noise_sigma.reshape(owned, LANES))
    forces, mean = pl.pallas_call(
        functools.partial(force_kernel, listed),
        in_specs=[pl.BlockSpec(memory_space=pl.ANY), far, far, whole, whole, whole],
        out_specs=[whole, far],
        out_shape=[
            jax.ShapeDtypeStruct(x.shape, f32),
            jax.ShapeDtypeStruct((owned, LANES), f32),
        ],
        scratch_shapes=[
            VMEM((IN_SLOTS, listed * LANES, LANES), f32),
            pltpu.SemaphoreType.DMA((IN_SLOTS,)),
            pltpu.SMEM((entries,), i32),
            VMEM(x.shape, f32),
            VMEM((listed, 4, 8, LANES), f32),
            VMEM((4, LANES, LANES), f32),
            pltpu.SemaphoreType.DMA((3,)),
        ],
        compiler_params=pltpu.CompilerParams(vmem_limit_bytes=57 << 20),
        name="forces",
    )(pos, x, g, ret.reshape(domains * CAPACITY, LANES), table, mean)
    return (mean.reshape(-1), forces.transpose(1, 0, 2))


def solution(mesh):
    return jax.shard_map(
        shards,
        mesh=mesh,
        in_specs=(
            P("rep", None, "dom"),
            P("dom"),
            P("dom"),
            P("dom"),
            P("dom", None),
            P(),
            P(),
            P(),
            P(),
            P("dom"),
            P("dom"),
        ),
        out_specs=(P("dom"), P("rep", None, "dom")),
        check_vma=False,
    )
```

profile of v0, /device:TPU:1, one launch (start us, length us, event | category | flops | bytes accessed | tf_op | source)
XLA Modules:
  0.0 82.4 jit_solution(13300255094726223002)
XLA Ops:
  0.6 0.8 copy.13
  1.4 0.7 reshape.31.lst_h
  2.1 23.9 %pairs.1 = (f32[8,72,128]{2,1,0:T(8,128)}, s32[512]{0:T(512)}, f32[512,4,128]{2,1,0:T(4,128)}, f32[32,2048,128]{2,1,0:T(8,128)}) custom-call(s32[32]{0:T(128)} %live_h.1, s32[512]{0:T(512)} %reshape.31.lst_h, s32[2048]{0:T(1024)} %owner_h.1, f32[3,1,4096]{2,1,0:T(1,128)} %bitcast.13, f32[32,128]{1,0:T(8,128)} %bitcast.17, f32[32,128]{1,0:T(8,128)} %bitcast.18, ...), custom_call_target="tpu_custom_call" | custom-call | tf_op jit(solution)/shard_map/pairs/pallas_call | solution.py:318
  25.9 29.7 %exchange.1 = (f32[256,128]{1,0:T(8,128)}, f32[8,64,128]{2,1,0:T(8,128)}) custom-call(f32[8,72,128]{2,1,0:T(8,128)} %get-tuple-element.12.send_ref, f32[256,128]{1,0:T(8,128)} %bitcast.15, f32[256,128]{1,0:T(8,128)} %bitcast.16), custom_call_target="tpu_custom_call" | custom-call | tf_op jit(solution)/shard_map/exchange/pallas_call | solution.py:353
  55.7 26.7 %forces.1 = (f32[3,1,4096]{2,1,0:T(1,128)}, f32[256,128]{1,0:T(8,128)}) custom-call(s32[512]{0:T(512)} %get-tuple-element.10.pos_h, f32[3,1,4096]{2,1,0:T(1,128)} %bitcast.14, f32[32,2048,128]{2,1,0:T(8,128)} %get-tuple-element.11.g_h, f32[512,128]{1,0:T(8,128)} %bitcast.12, f32[512,4,128]{2,1,0:T(4,128)} %get-tuple-element.14.table_ref, ...), custom_call_target="tpu_custom_call" | custom-call | tf_op jit(solution)/shard_map/forces/pallas_call | solution.py:382
where the time goes:
time: 83.2 us; the launch traced here: 82.4 us
  Pallas kernels  80.3 us (97%)
  local copies, waits for them, and re-layouts  1.43 us (2%)
    pallas_call x1, Pallas kernels, shards(): pl.pallas_call(functools.partial(exchange_kernel, domains, replicas), in_...  29.7 us
    pallas_call x1, Pallas kernels, shards(): pl.pallas_call(functools.partial(force_kernel, listed), in_specs=[pl.Bloc...  26.7 us
    pallas_call x1, Pallas kernels, shards(): pl.pallas_call(functools.partial(pair_kernel, listed, owned), in_specs=[f...  23.9 us

commit v1 on v0

v1 whole, which is shorter than its diff:
```python
import functools
import math

import jax
import jax.numpy as jnp
from jax import lax
from jax.experimental import pallas as pl
from jax.experimental.pallas import tpu as pltpu
from jax.sharding import PartitionSpec as P

CAPACITY = 64
LANES = 128
STRIP = 16
ROWS = 64

energy_unit = 2.494
norm = (2.0 * math.pi) ** -1.5
half_log2e = -0.5 / math.log(2.0)
dead = -1.0e4
VMEM = pltpu.VMEM
SMEM = pltpu.SMEM
MESH = pl.DeviceIdType.MESH
f32, i32, bf16 = jnp.float32, jnp.int32, jnp.bfloat16


def split(value):
    second = value - value.astype(bf16).astype(f32)
    third = second - second.astype(bf16).astype(f32)
    return value, second, third


def pieces_of(value):
    return [piece.astype(bf16) for piece in split(value)]


def dot3(picks, value):
    total = None
    for piece in pieces_of(value):
        part = jnp.dot(picks, piece, preferred_element_type=f32)
        total = part if total is None else total + part
    return total


def iota(shape, axis):
    return lax.broadcasted_iota(i32, shape, axis)


def splat_rows(tile):
    return jnp.transpose(tile)


def step_kernel(
    replicas, domains, blocks, listed, owned,
    live_h, lst_h, owner_h, x_h, av_h, aw_h, m_h, cv_h, cw_h, target_h, sigma_h,
    f_ref, mean_ref,
    live, lst, owner, x_v, av_v, aw_v, m_v, cv_v, cw_v, target_v, sigma_v,
    g_v, lhs_s, avt_s, rhs_s, part, dev_s, slot_s, perm_a, perm_b, slot_send, slot_land,
    out_send, out_land, back_send, back_land, ret, adj_e, mean_send, mean_land, sums,
    loads, slot_ss, slot_rs, out_ss, out_rs, back_ss, back_rs, mean_ss, mean_rs,
):
    me_r = lax.axis_index("rep")
    me_d = lax.axis_index("dom")
    entries = blocks * listed
    slots = domains * CAPACITY
    width = LANES // replicas
    slab = CAPACITY // replicas
    per = LANES // CAPACITY
    devices = replicas * domains
    chunk = owned // replicas
    fetches = [
        pltpu.make_async_copy(src, dst, loads.at[i])
        for i, (src, dst) in enumerate(
            [(lst_h, lst), (owner_h, owner), (live_h, live), (x_h, x_v), (av_h, av_v), (aw_h, aw_v),
             (m_h, m_v), (cv_h, cv_v), (cw_h, cw_v), (target_h, target_v), (sigma_h, sigma_v)]
        )
    ]
    for fetch in fetches:
        fetch.start()
    barrier = pltpu.get_barrier_semaphore()

    def peer(s):
        return lax.rem(me_r + s // domains, replicas), lax.rem(me_d + lax.rem(s, domains), domains)

    def greet(s, carry):
        pl.semaphore_signal(barrier, inc=1, device_id=peer(s), device_id_type=MESH)
        return carry

    lax.fori_loop(1, devices, greet, 0)
    for fetch in fetches[:6]:
        fetch.wait()

    lane = iota((1, LANES), 1)
    group = lane // width
    one = jnp.ones((1, LANES), f32)
    zero = jnp.zeros((1, LANES), f32)

    def places(a, carry):
        for k in range(listed):
            place = owner[lst[k, a]]
            dev = lax.div(place, owned)
            e = a * listed + k
            dev_s[pl.ds(e, 1), :] = jnp.full((1, LANES), dev, i32)
            slot_s[pl.ds(e, 1), :] = jnp.full((1, LANES), place - dev * owned + 1, i32)
        return carry

    lax.fori_loop(0, blocks, places, 0)
    dev = dev_s[...]
    hot = jnp.where(dev == lane, 1.0, 0.0)
    before = jnp.where(iota((entries, entries), 1) < iota((entries, entries), 0), 1.0, 0.0).astype(bf16)
    rank = jnp.dot(before, hot.astype(bf16), preferred_element_type=f32)
    rank = jnp.sum(rank * hot, axis=1, keepdims=True)
    place = dev * CAPACITY + jnp.broadcast_to(rank, (entries, LANES)).astype(i32)
    for j in range(slots // LANES):
        perm_b[:, j * LANES : (j + 1) * LANES] = jnp.where(place == lane + j * LANES, 1.0, 0.0).astype(bf16)
    place_f = place.astype(f32)
    for j in range(entries // LANES):
        row = jnp.transpose(place_f[j * LANES : (j + 1) * LANES])[0:1].astype(i32)
        perm_a[:, j * LANES : (j + 1) * LANES] = jnp.where(
            iota((slots, LANES), 0) == row, 1.0, 0.0
        ).astype(bf16)
    slot_c = jnp.dot(perm_a[...], slot_s[...].astype(f32).astype(bf16), preferred_element_type=f32)
    for j in range(slots // LANES):
        slot_send[j] = jnp.transpose(slot_c[j * LANES : (j + 1) * LANES])[0:8]
    pl.semaphore_wait(barrier, devices - 1)

    def slot_copy(s):
        to = lax.rem(me_d + s, domains)
        return pltpu.make_async_remote_copy(
            src_ref=slot_send.at[to // per], dst_ref=slot_land.at[s],
            send_sem=slot_ss.at[s], recv_sem=slot_rs.at[s],
            device_id=(me_r, to), device_id_type=MESH,
        )

    for s in range(1, domains):
        slot_copy(s).start()
    slot_land[0] = slot_send[me_d // per]

    for fetch in fetches[6:]:
        fetch.wait()
    none = jnp.zeros((8, LANES), f32)

    def prepare(a):
        turn = lax.rem(a, 2)
        x = jnp.concatenate(
            [x_v[c, :, pl.ds(pl.multiple_of(a * LANES, LANES), LANES)] for c in range(3)], axis=0
        )
        xx = jnp.sum(x * x, axis=0, keepdims=True)
        av = av_v[pl.ds(a, 1), :]
        lw = jnp.where(lane < live[a], jnp.log2(aw_v[pl.ds(a, 1), :]), dead)
        left = jnp.concatenate(
            [half_log2e * -2.0 * x, half_log2e * one, half_log2e * xx + av * lw, lw, zero, zero], axis=0
        )
        l0, l1, l2 = split(left)
        big = jnp.concatenate([l0, l0, l1, l1, l0, l2, none, none], axis=0)
        lhs_s[turn] = jnp.transpose(big.astype(bf16))
        avt_s[turn] = jnp.transpose(jnp.broadcast_to(av, (LANES, LANES)))
        for k in range(listed):
            b = lst[k, a]
            m = m_v[b]
            mm = jnp.sum(m * m, axis=0, keepdims=True)
            r0, r1, r2 = split(jnp.concatenate([m, mm, one, cv_v[b], zero, zero], axis=0))
            here = slice((k % 2) * LANES, (k % 2 + 1) * LANES)
            rhs_s[turn, k // 2, 0:16, here] = jnp.concatenate([r0, r1], axis=0).astype(bf16)
            rhs_s[turn, k // 2, 16:32, here] = jnp.concatenate([r2, r0], axis=0).astype(bf16)

    blank = jnp.zeros((16, 2 * LANES), bf16)

    def pairs(a, carry):
        turn = lax.rem(a, 2)
        lhs = lhs_s[turn]
        for k in range(0, listed, 2):
            upper, lower = rhs_s[turn, k // 2, 0:16], rhs_s[turn, k // 2, 16:32]
            rhs = jnp.concatenate([upper, upper, lower, blank], axis=0)
            scaled = jnp.dot(lhs, rhs, preferred_element_type=f32)
            for i in range(2):
                e = a * listed + k + i
                b = lst[k + i, a]
                cv = jnp.broadcast_to(cv_v[b], (8, LANES))
                total = jnp.zeros((8, LANES), f32)
                for h in range(0, LANES, 8):
                    root = lax.rsqrt(avt_s[turn, h : h + 8, :] + cv)
                    inv = root * root
                    ov = (root * inv) * jnp.exp2(scaled[h : h + 8, i * LANES : (i + 1) * LANES] * inv)
                    total = total + ov
                    g_v[e, h : h + 8, :] = ov * inv
                part[pl.ds(e, 1), :] = jnp.sum(total, axis=0, keepdims=True) * (norm * cw_v[b])
        prepare(lax.rem(a + 1, blocks))
        return carry

    prepare(0)
    lax.fori_loop(0, blocks, pairs, 0)

    def turned(pieces, to):
        total = None
        for g in range(replicas):
            shift = (width * (g - to)) % LANES
            piece = pltpu.roll(pieces[g], shift, axis=1) if shift else pieces[g]
            piece = jnp.where(group == g, piece, 0.0)
            total = piece if total is None else total + piece
        return total

    def fold(value):
        shift = width
        while shift < LANES:
            value = value + pltpu.roll(value, shift, axis=1)
            shift = 2 * shift
        return value

    placed = dot3(perm_a[...], part[...]).reshape(domains, replicas, slab, LANES)
    parts = [placed[:, g].reshape(domains * slab, LANES) for g in range(replicas)]
    for q in range(replicas):
        out_send[q] = turned(parts, q).reshape(domains, slab, LANES)

    def out_copy(s):
        to_r, to_d = peer(s)
        return pltpu.make_async_remote_copy(
            src_ref=out_send.at[to_r, to_d], dst_ref=out_land.at[s],
            send_sem=out_ss.at[s], recv_sem=out_rs.at[s],
            device_id=(to_r, to_d), device_id_type=MESH,
        )

    def start_out(s, carry):
        out_copy(s).start()
        return carry

    lax.fori_loop(1, devices, start_out, 0)
    out_land[0] = out_send[me_r, me_d]

    mine = group == me_r
    wanted = fold(jnp.where(mine, target_v[...], 0.0))
    sigmas = fold(jnp.where(mine, sigma_v[...], 0.0))
    for s in range(1, domains):
        slot_copy(s).wait_recv()
    odd = lax.rem(me_d, per)
    rows = []
    for j in range(domains // per):
        total = None
        for i in range(per):
            tile = slot_land[j * per + i]
            moved = None
            for n in range(per):
                shift = ((i - n) * CAPACITY) % LANES
                option = pltpu.roll(tile, shift, axis=1) if shift else tile
                moved = option if moved is None else jnp.where(odd == n, option, moved)
            moved = jnp.where(lane // CAPACITY == i, moved, 0.0)
            total = moved if total is None else total + moved
        rows.append(total[0:1].astype(i32))
    picks = jnp.concatenate(
        [jnp.where(iota((owned, LANES), 0) + 1 == row, 1.0, 0.0).astype(bf16) for row in rows], axis=1
    )

    def wait_out(s, carry):
        out_copy(s).wait_recv()
        return carry

    lax.fori_loop(1, devices, wait_out, 0)
    spread = []
    for s in range(domains):
        total = out_land[s]
        for r in range(1, replicas):
            total = total + out_land[r * domains + s]
        for g in range(replicas):
            spread.append(jnp.where(group == g, total, 0.0))
    mean = fold(dot3(picks, jnp.concatenate(spread, axis=0))) / replicas
    misfit = mean - wanted
    adjoint = misfit / (sigmas * sigmas + 0.5 * misfit * misfit) / replicas
    adjoints = pieces_of(adjoint)
    for s in range(domains):
        value = None
        for piece in adjoints:
            one_part = lax.dot_general(
                picks[:, (s // per) * LANES : (s // per + 1) * LANES], piece,
                (((0,), (0,)), ((), ())), preferred_element_type=f32,
            )[(s % per) * CAPACITY : (s % per + 1) * CAPACITY]
            value = one_part if value is None else value + one_part
        packed = None
        for g in range(replicas):
            piece = jnp.where(group == g, value[g * slab : (g + 1) * slab], 0.0)
            packed = piece if packed is None else packed + piece
        back_send[s] = packed

    def back_copy(n):
        s = lax.rem(n, domains)
        to = lax.rem(me_r + n // domains, replicas), lax.rem(me_d + domains - s, domains)
        return pltpu.make_async_remote_copy(
            src_ref=back_send.at[s], dst_ref=back_land.at[n],
            send_sem=back_ss.at[n], recv_sem=back_rs.at[n],
            device_id=to, device_id_type=MESH,
        )

    def start_back(n, carry):
        back_copy(n).start()
        return carry

    lax.fori_loop(1, devices, start_back, 0)
    back_land[0] = back_send[0]
    packed = None
    for g in range(replicas):
        piece = jnp.where(group == g, mean[g * chunk : (g + 1) * chunk], 0.0)
        packed = piece if packed is None else packed + piece
    mean_send[...] = packed

    def mean_copy(n):
        return pltpu.make_async_remote_copy(
            src_ref=mean_send, dst_ref=mean_land.at[n],
            send_sem=mean_ss.at[n], recv_sem=mean_rs.at[n],
            device_id=(lax.rem(me_r + n, replicas), me_d), device_id_type=MESH,
        )

    for n in range(1, replicas):
        mean_copy(n).start()
    mean_land[0] = packed

    def wait_back(n, carry):
        back_copy(n).wait_recv()
        return carry

    lax.fori_loop(1, devices, wait_back, 0)
    source = [lax.rem(me_r + replicas - q, replicas) for q in range(replicas)]
    for s in range(domains):
        messages = [back_land[source[q] * domains + s] for q in range(replicas)]
        ret[lax.rem(me_d + s, domains)] = jnp.concatenate(
            [turned(messages, g) for g in range(replicas)], axis=0
        )
    adj_e[...] = dot3(perm_b[...], ret[...].reshape(slots, LANES))
    ones = jnp.ones((8, LANES), f32)

    def forces(a, carry):
        coefs = []
        for k in range(listed):
            b = lst[k, a]
            scale = (energy_unit * norm) * cw_v[b] * adj_e[pl.ds(a * listed + k, 1), :]
            m = m_v[b]
            sums[4, k * 4 : k * 4 + 4, :] = jnp.concatenate([scale, m * scale], axis=0)
        for h in range(0, LANES, STRIP):
            acc = [[jnp.zeros((8, LANES), f32) for _ in range(STRIP // 8)] for _ in range(4)]
            for k in range(listed):
                rows = [
                    jnp.broadcast_to(sums[4, k * 4 + c : k * 4 + c + 1, :], (8, LANES)) for c in range(4)
                ]
                for q in range(STRIP // 8):
                    g = g_v[a * listed + k, h + q * 8 : h + q * 8 + 8, :]
                    for c in range(4):
                        acc[c][q] = acc[c][q] + g * rows[c]
            for c in range(4):
                for q in range(STRIP // 8):
                    sums[c, h + q * 8 : h + q * 8 + 8, :] = acc[c][q]
        flat = [
            lax.dot_general(
                ones, sums[c], (((1,), (1,)), ((), ())), precision=lax.Precision.HIGHEST,
                preferred_element_type=f32,
            )[0:1]
            for c in range(4)
        ]
        here = pl.ds(pl.multiple_of(a * LANES, LANES), LANES)
        for c in range(3):
            f_ref[c, :, here] = x_v[c, :, here] * flat[0] - flat[c + 1]
        return carry

    lax.fori_loop(0, blocks, forces, 0)
    for n in range(1, replicas):
        mean_copy(n).wait_recv()
    messages = [mean_land[source[q]] for q in range(replicas)]
    for g in range(replicas):
        mean_ref[g * chunk : (g + 1) * chunk, :] = turned(messages, g)

    def sent(s, carry):
        out_copy(s).wait_send()
        back_copy(s).wait_send()
        return carry

    lax.fori_loop(1, devices, sent, 0)
    for s in range(1, domains):
        slot_copy(s).wait_send()
    for n in range(1, replicas):
        mean_copy(n).wait_send()


def shards(
    coords, atom_var, atom_weight, atoms_live, block_list, owner_map,
    comp_means, comp_var, comp_weight, target, noise_sigma,
):
    replicas = lax.axis_size("rep")
    domains = lax.axis_size("dom")
    blocks, listed = block_list.shape
    comp_blocks = owner_map.shape[0]
    owned = target.shape[0] // LANES
    entries = blocks * listed
    slots = domains * CAPACITY
    devices = domains * replicas
    slab = CAPACITY // replicas
    per = LANES // CAPACITY
    x = coords.transpose(1, 0, 2)
    cm = comp_means.reshape(3, comp_blocks, LANES).transpose(1, 0, 2)
    cv = comp_var.reshape(comp_blocks, 1, LANES)
    cw = comp_weight.reshape(comp_blocks, 1, LANES)
    whole = pl.BlockSpec(memory_space=VMEM)
    far = pl.BlockSpec(memory_space=pltpu.HBM)
    dma = pltpu.SemaphoreType.DMA
    forces, mean = pl.pallas_call(
        functools.partial(step_kernel, replicas, domains, blocks, listed, owned),
        in_specs=[far] * 11,
        out_specs=[whole] * 2,
        out_shape=[
            jax.ShapeDtypeStruct(x.shape, f32),
            jax.ShapeDtypeStruct((owned, LANES), f32),
        ],
        scratch_shapes=[
            SMEM((blocks,), i32),
            SMEM((listed, blocks), i32),
            SMEM((comp_blocks,), i32),
            VMEM(x.shape, f32),
            VMEM((blocks, LANES), f32),
            VMEM((blocks, LANES), f32),
            VMEM(cm.shape, f32),
            VMEM(cv.shape, f32),
            VMEM(cw.shape, f32),
            VMEM((owned, LANES), f32),
            VMEM((owned, LANES), f32),
            VMEM((entries, LANES, LANES), f32),
            VMEM((2, LANES, ROWS), bf16),
            VMEM((2, LANES, LANES), f32),
            VMEM((2, listed // 2, 32, 2 * LANES), bf16),
            VMEM((entries, LANES), f32),
            VMEM((entries, LANES), i32),
            VMEM((entries, LANES), i32),
            VMEM((slots, entries), bf16),
            VMEM((entries, slots), bf16),
            VMEM((slots // LANES, 8, LANES), f32),
            VMEM((domains, 8, LANES), f32),
            VMEM((replicas, domains, slab, LANES), f32),
            VMEM((devices, slab, LANES), f32),
            VMEM((domains, slab, LANES), f32),
            VMEM((devices, slab, LANES), f32),
            VMEM((domains, CAPACITY, LANES), f32),
            VMEM((entries, LANES), f32),
            VMEM((owned // replicas, LANES), f32),
            VMEM((replicas, owned // replicas, LANES), f32),
            VMEM((5, LANES, LANES), f32),
            dma((11,)),
            dma((domains,)),
            dma((domains,)),
            dma((devices,)),
            dma((devices,)),
            dma((devices,)),
            dma((devices,)),
            dma((replicas,)),
            dma((replicas,)),
        ],
        compiler_params=pltpu.CompilerParams(
            collective_id=0, has_side_effects=True, vmem_limit_bytes=60 << 20
        ),
        name="step",
    )(
        atoms_live, block_list.T, owner_map, x,
        atom_var.reshape(blocks, LANES), atom_weight.reshape(blocks, LANES),
        cm, cv, cw, target.reshape(owned, LANES), noise_sigma.reshape(owned, LANES),
    )
    return (mean.reshape(-1), forces.transpose(1, 0, 2))


def solution(mesh):
    return jax.shard_map(
        shards,
        mesh=mesh,
        in_specs=(
            P("rep", None, "dom"),
            P("dom"),
            P("dom"),
            P("dom"),
            P("dom", None),
            P(),
            P(),
            P(),
            P(),
            P("dom"),
            P("dom"),
        ),
        out_specs=(P("dom"), P("rep", None, "dom")),
        check_vma=False,
    )
```

time: 83.2 us -> 71.3 us (0.86)
  Pallas kernels: 80.3 us -> 67.5 us
  local copies, waits for them, and re-layouts: 1.43 us -> 2.99 us
    pallas_call x3 -> x1, Pallas kernels: 80.3 us -> 67.5 us  [shards(): pl.pallas_call(functools.partial(step_kernel, replicas, domains, blocks,...]
    unnamed x1 -> x2, local copies, waits for them, and re-layouts: 0.77 us -> 2.99 us
where the time goes in v1:
time: 71.3 us; the launch traced here: 71.1 us
  Pallas kernels  67.5 us (95%)
  local copies, waits for them, and re-layouts  2.99 us (4%)
    pallas_call x1, Pallas kernels, shards(): pl.pallas_call(functools.partial(step_kernel, replicas, domains, blocks,...  67.5 us
    unnamed x2, local copies, waits for them, and re-layouts  2.99 us

profile of v1, /device:TPU:1, one launch (start us, length us, event | category | flops | bytes accessed | tf_op | source)
XLA Modules:
  0.0 71.1 jit_solution(5860380625822863629)
XLA Ops:
  0.6 67.5 %step.1 = (f32[3,1,4096]{2,1,0:T(1,128)}, f32[256,128]{1,0:T(8,128)}) custom-call(s32[32]{0:T(128)} %live_h.1, s32[16,32]{1,0:T(8,128)} %bitcast.23, s32[2048]{0:T(1024)} %owner_h.1, f32[3,1,4096]{2,1,0:T(1,128)} %bitcast.19, f32[32,128]{1,0:T(8,128)} %bitcast.21, f32[32,128]{1,0:T(8,128)} %bitcast.22, f32[2048,3,128]{2,1,0:T(4,128)} %bitcast.13, ...), custom_call_target="tpu_custom_call" | custom-call | tf_op jit(solution)/shard_map/step/pallas_call | solution.py:400
  68.2 1.6 %copy.15 = f32[32768]{0:T(1024)} copy(f32[32768]{0:T(1024)} %bitcast.16) | data formatting | bytes 262144
  69.7 1.4 %copy.16 = f32[1,3,4096]{2,0,1:T(1,128)} copy(f32[1,3,4096]{2,0,1:T(1,128)} %bitcast.20) | data formatting | bytes 98304

commit v2 on v1

--- a/solution.py
+++ b/solution.py
@@ -45,17 +45,13 @@
     return lax.broadcasted_iota(i32, shape, axis)
 
 
-def splat_rows(tile):
-    return jnp.transpose(tile)
-
-
 def step_kernel(
     replicas, domains, blocks, listed, owned,
     live_h, lst_h, owner_h, x_h, av_h, aw_h, m_h, cv_h, cw_h, target_h, sigma_h,
     f_ref, mean_ref,
     live, lst, owner, x_v, av_v, aw_v, m_v, cv_v, cw_v, target_v, sigma_v,
     g_v, lhs_s, avt_s, rhs_s, part, dev_s, slot_s, perm_a, perm_b, slot_send, slot_land,
-    out_send, out_land, back_send, back_land, ret, adj_e, mean_send, mean_land, sums,
+    out_send, out_land, back_send, back_land, ret, adj_e, mean_send, mean_land, sums, coefs,
     loads, slot_ss, slot_rs, out_ss, out_rs, back_ss, back_rs, mean_ss, mean_rs,
 ):
     me_r = lax.axis_index("rep")
@@ -323,20 +319,24 @@
             [turned(messages, g) for g in range(replicas)], axis=0
         )
     adj_e[...] = dot3(perm_b[...], ret[...].reshape(slots, LANES))
-    ones = jnp.ones((8, LANES), f32)
+    def finish(a):
+        turn = lax.rem(a, 2)
+        flat = [jnp.sum(jnp.transpose(sums[turn, c]), axis=0, keepdims=True) for c in range(4)]
+        here = pl.ds(pl.multiple_of(a * LANES, LANES), LANES)
+        for c in range(3):
+            f_ref[c, :, here] = x_v[c, :, here] * flat[0] - flat[c + 1]
 
     def forces(a, carry):
-        coefs = []
+        turn = lax.rem(a, 2)
         for k in range(listed):
             b = lst[k, a]
             scale = (energy_unit * norm) * cw_v[b] * adj_e[pl.ds(a * listed + k, 1), :]
-            m = m_v[b]
-            sums[4, k * 4 : k * 4 + 4, :] = jnp.concatenate([scale, m * scale], axis=0)
+            coefs[k * 4 : k * 4 + 4, :] = jnp.concatenate([scale, m_v[b] * scale], axis=0)
         for h in range(0, LANES, STRIP):
             acc = [[jnp.zeros((8, LANES), f32) for _ in range(STRIP // 8)] for _ in range(4)]
             for k in range(listed):
                 rows = [
-                    jnp.broadcast_to(sums[4, k * 4 + c : k * 4 + c + 1, :], (8, LANES)) for c in range(4)
+                    jnp.broadcast_to(coefs[k * 4 + c : k * 4 + c + 1, :], (8, LANES)) for c in range(4)
                 ]
                 for q in range(STRIP // 8):
                     g = g_v[a * listed + k, h + q * 8 : h + q * 8 + 8, :]
@@ -344,20 +344,13 @@
                         acc[c][q] = acc[c][q] + g * rows[c]
             for c in range(4):
                 for q in range(STRIP // 8):
-                    sums[c, h + q * 8 : h + q * 8 + 8, :] = acc[c][q]
-        flat = [
-            lax.dot_general(
-                ones, sums[c], (((1,), (1,)), ((), ())), precision=lax.Precision.HIGHEST,
-                preferred_element_type=f32,
-            )[0:1]
-            for c in range(4)
-        ]
-        here = pl.ds(pl.multiple_of(a * LANES, LANES), LANES)
-        for c in range(3):
-            f_ref[c, :, here] = x_v[c, :, here] * flat[0] - flat[c + 1]
-        return carry
-
+                    sums[turn, c, h + q * 8 : h + q * 8 + 8, :] = acc[c][q]
+        finish(lax.rem(a + blocks - 1, blocks))
+        return carry
+
+    sums[(blocks - 1) % 2] = jnp.zeros((4, LANES, LANES), f32)
     lax.fori_loop(0, blocks, forces, 0)
+    finish(blocks - 1)
     for n in range(1, replicas):
         mean_copy(n).wait_recv()
     messages = [mean_land[source[q]] for q in range(replicas)]
@@ -374,6 +367,17 @@
         slot_copy(s).wait_send()
     for n in range(1, replicas):
         mean_copy(n).wait_send()
+
+
+def hand_over(f_h, mean_h, f_out, mean_out, sems):
+    copies = [
+        pltpu.make_async_copy(f_h, f_out, sems.at[0]),
+        pltpu.make_async_copy(mean_h, mean_out, sems.at[1]),
+    ]
+    for copy in copies:
+        copy.start()
+    for copy in copies:
+        copy.wait()
 
 
 def shards(
@@ -436,7 +440,8 @@
             VMEM((entries, LANES), f32),
             VMEM((owned // replicas, LANES), f32),
             VMEM((replicas, owned // replicas, LANES), f32),
-            VMEM((5, LANES, LANES), f32),
+            VMEM((2, 4, LANES, LANES), f32),
+            VMEM((4 * listed, LANES), f32),
             dma((11,)),
             dma((domains,)),
             dma((domains,)),
@@ -456,6 +461,17 @@
         atom_var.reshape(blocks, LANES), atom_weight.reshape(blocks, LANES),
         cm, cv, cw, target.reshape(owned, LANES), noise_sigma.reshape(owned, LANES),
     )
+    forces, mean = pl.pallas_call(
+        hand_over,
+        in_specs=[far] * 2,
+        out_specs=[far] * 2,
+        out_shape=[
+            jax.ShapeDtypeStruct(x.shape, f32),
+            jax.ShapeDtypeStruct((owned, LANES), f32),
+        ],
+        scratch_shapes=[dma((2,))],
+        name="hand_over",
+    )(forces, mean)
     return (mean.reshape(-1), forces.transpose(1, 0, 2))
 
 

time: 71.3 us -> 63.7 us (0.89)
  Pallas kernels: 67.5 us -> 62.9 us
  local copies, waits for them, and re-layouts: 2.99 us -> 0 us
    pallas_call x1, Pallas kernels: 67.5 us -> 56.3 us  [shards(): pl.pallas_call(functools.partial(step_kernel, replicas, domains, blocks,...]
    pallas_call x0 -> x1, Pallas kernels: none -> 6.58 us  [shards(): pl.pallas_call(hand_over, in_specs=[far] * 2, out_specs=[far] * 2, out_sh...]
    unnamed x2 -> x0, local copies, waits for them, and re-layouts: 2.99 us -> none
where the time goes in v2:
time: 63.7 us; the launch traced here: 63.5 us
  Pallas kernels  62.9 us (99%)
  between operations  0.64 us (1%)
    pallas_call x1, Pallas kernels, shards(): pl.pallas_call(functools.partial(step_kernel, replicas, domains, blocks,...  56.3 us
    pallas_call x1, Pallas kernels, shards(): pl.pallas_call(hand_over, in_specs=[far] * 2, out_specs=[far] * 2, out_sh...  6.58 us

profile of v2, /device:TPU:1, one launch (start us, length us, event | category | flops | bytes accessed | tf_op | source)
XLA Modules:
  0.0 63.5 jit_solution(11770646091120850913)
XLA Ops:
  0.6 56.3 %step.1 = (f32[3,1,4096]{2,1,0:T(1,128)}, f32[256,128]{1,0:T(8,128)}) custom-call(s32[32]{0:T(128)} %live_h.1, s32[16,32]{1,0:T(8,128)} %bitcast.21, s32[2048]{0:T(1024)} %owner_h.1, f32[3,1,4096]{2,1,0:T(1,128)} %bitcast.18, f32[32,128]{1,0:T(8,128)} %bitcast.19, f32[32,128]{1,0:T(8,128)} %bitcast.20, f32[2048,3,128]{2,1,0:T(4,128)} %bitcast.13, ...), custom_call_target="tpu_custom_call" | custom-call | tf_op jit(solution)/shard_map/step/pallas_call | solution.py:404
  57.0 6.6 %hand_over.1 = (f32[3,1,4096]{2,1,0:T(1,128)}, f32[256,128]{1,0:T(8,128)}) custom-call(f32[3,1,4096]{2,1,0:T(1,128)} %get-tuple-element.6.f_h, f32[256,128]{1,0:T(8,128)} %get-tuple-element.7.mean_h), custom_call_target="tpu_custom_call" | custom-call | tf_op jit(solution)/shard_map/hand_over/pallas_call | solution.py:464

commit v3 on v2

--- a/solution.py
+++ b/solution.py
@@ -10,7 +10,7 @@
 
 CAPACITY = 64
 LANES = 128
-STRIP = 16
+STRIP = 32
 ROWS = 64
 
 energy_unit = 2.494
@@ -46,12 +46,12 @@
 
 
 def step_kernel(
-    replicas, domains, blocks, listed, owned,
+    replicas, domains, blocks, listed, owned, dense,
     live_h, lst_h, owner_h, x_h, av_h, aw_h, m_h, cv_h, cw_h, target_h, sigma_h,
     f_ref, mean_ref,
     live, lst, owner, x_v, av_v, aw_v, m_v, cv_v, cw_v, target_v, sigma_v,
-    g_v, lhs_s, avt_s, rhs_s, part, dev_s, slot_s, perm_a, perm_b, slot_send, slot_land,
-    out_send, out_land, back_send, back_land, ret, adj_e, mean_send, mean_land, sums, coefs,
+    g_v, lhs_s, avt_s, rhs_s, part, place_s, perm_a, perm_b, slot_send, slot_land,
+    out_send, out_land, back_send, back_land, ret, adj_e, mean_send, mean_land, sums, coefs, gt_v, left_s, dense_s, back_picks,
     loads, slot_ss, slot_rs, out_ss, out_rs, back_ss, back_rs, mean_ss, mean_rs,
 ):
     me_r = lax.axis_index("rep")
@@ -92,15 +92,12 @@
 
     def places(a, carry):
         for k in range(listed):
-            place = owner[lst[k, a]]
-            dev = lax.div(place, owned)
-            e = a * listed + k
-            dev_s[pl.ds(e, 1), :] = jnp.full((1, LANES), dev, i32)
-            slot_s[pl.ds(e, 1), :] = jnp.full((1, LANES), place - dev * owned + 1, i32)
+            place_s[pl.ds(a * listed + k, 1), :] = jnp.full((1, LANES), owner[lst[k, a]], i32)
         return carry
 
     lax.fori_loop(0, blocks, places, 0)
-    dev = dev_s[...]
+    dev = lax.div(place_s[...], owned)
+    slot = place_s[...] - dev * owned + 1
     hot = jnp.where(dev == lane, 1.0, 0.0)
     before = jnp.where(iota((entries, entries), 1) < iota((entries, entries), 0), 1.0, 0.0).astype(bf16)
     rank = jnp.dot(before, hot.astype(bf16), preferred_element_type=f32)
@@ -114,10 +111,9 @@
         perm_a[:, j * LANES : (j + 1) * LANES] = jnp.where(
             iota((slots, LANES), 0) == row, 1.0, 0.0
         ).astype(bf16)
-    slot_c = jnp.dot(perm_a[...], slot_s[...].astype(f32).astype(bf16), preferred_element_type=f32)
+    slot_c = jnp.dot(perm_a[...], slot.astype(f32).astype(bf16), preferred_element_type=f32)
     for j in range(slots // LANES):
         slot_send[j] = jnp.transpose(slot_c[j * LANES : (j + 1) * LANES])[0:8]
-    pl.semaphore_wait(barrier, devices - 1)
 
     def slot_copy(s):
         to = lax.rem(me_d + s, domains)
@@ -127,16 +123,11 @@
             device_id=(me_r, to), device_id_type=MESH,
         )
 
-    for s in range(1, domains):
-        slot_copy(s).start()
-    slot_land[0] = slot_send[me_d // per]
-
     for fetch in fetches[6:]:
         fetch.wait()
     none = jnp.zeros((8, LANES), f32)
 
-    def prepare(a):
-        turn = lax.rem(a, 2)
+    def prepare(a, turn):
         x = jnp.concatenate(
             [x_v[c, :, pl.ds(pl.multiple_of(a * LANES, LANES), LANES)] for c in range(3)], axis=0
         )
@@ -161,8 +152,7 @@
 
     blank = jnp.zeros((16, 2 * LANES), bf16)
 
-    def pairs(a, carry):
-        turn = lax.rem(a, 2)
+    def pair_block(a, turn):
         lhs = lhs_s[turn]
         for k in range(0, listed, 2):
             upper, lower = rhs_s[turn, k // 2, 0:16], rhs_s[turn, k // 2, 16:32]
@@ -180,11 +170,21 @@
                     total = total + ov
                     g_v[e, h : h + 8, :] = ov * inv
                 part[pl.ds(e, 1), :] = jnp.sum(total, axis=0, keepdims=True) * (norm * cw_v[b])
-        prepare(lax.rem(a + 1, blocks))
-        return carry
-
-    prepare(0)
-    lax.fori_loop(0, blocks, pairs, 0)
+        prepare(lax.rem(a + 1, blocks), 1 - turn)
+
+    def pairs(n, carry):
+        pair_block(2 * n, 0)
+        pair_block(2 * n + 1, 1)
+        return carry
+
+    prepare(0, 0)
+    early = blocks // 8
+    lax.fori_loop(0, early, pairs, 0)
+    pl.semaphore_wait(barrier, devices - 1)
+    for s in range(1, domains):
+        slot_copy(s).start()
+    slot_land[0] = slot_send[me_d // per]
+    lax.fori_loop(early, blocks // 2, pairs, 0)
 
     def turned(pieces, to):
         total = None
@@ -221,6 +221,15 @@
 
     lax.fori_loop(1, devices, start_out, 0)
     out_land[0] = out_send[me_r, me_d]
+
+    def convert(a, carry):
+        for k in range(dense):
+            turned_g = jnp.transpose(g_v[a * listed + listed - dense + k])
+            high = turned_g.astype(bf16)
+            low = (turned_g - high.astype(f32)).astype(bf16)
+            gt_v[a, k * LANES : (k + 1) * LANES, 0:LANES] = high
+            gt_v[a, k * LANES : (k + 1) * LANES, LANES : 2 * LANES] = low
+        return carry
 
     mine = group == me_r
     wanted = fold(jnp.where(mine, target_v[...], 0.0))
@@ -240,10 +249,19 @@
                 moved = option if moved is None else jnp.where(odd == n, option, moved)
             moved = jnp.where(lane // CAPACITY == i, moved, 0.0)
             total = moved if total is None else total + moved
-        rows.append(total[0:1].astype(i32))
+        rows.append(total[0:1])
     picks = jnp.concatenate(
-        [jnp.where(iota((owned, LANES), 0) + 1 == row, 1.0, 0.0).astype(bf16) for row in rows], axis=1
+        [jnp.where(iota((owned, LANES), 0) + 1 == row.astype(i32), 1.0, 0.0).astype(bf16) for row in rows],
+        axis=1,
     )
+    for j in range(domains // per):
+        column = jnp.transpose(jnp.broadcast_to(rows[j], (LANES, LANES))).astype(i32)
+        for i in range(max(1, owned // LANES)):
+            span = min(owned, LANES)
+            back_picks[j, :, i * span : (i + 1) * span] = jnp.where(
+                column[:, :span] == iota((1, span), 1) + (i * span + 1), 1.0, 0.0
+            ).astype(bf16)
+    lax.fori_loop(0, blocks // 2, convert, 0)
 
     def wait_out(s, carry):
         out_copy(s).wait_recv()
@@ -261,19 +279,18 @@
     misfit = mean - wanted
     adjoint = misfit / (sigmas * sigmas + 0.5 * misfit * misfit) / replicas
     adjoints = pieces_of(adjoint)
-    for s in range(domains):
+    for j in range(domains // per):
         value = None
         for piece in adjoints:
-            one_part = lax.dot_general(
-                picks[:, (s // per) * LANES : (s // per + 1) * LANES], piece,
-                (((0,), (0,)), ((), ())), preferred_element_type=f32,
-            )[(s % per) * CAPACITY : (s % per + 1) * CAPACITY]
-            value = one_part if value is None else value + one_part
-        packed = None
-        for g in range(replicas):
-            piece = jnp.where(group == g, value[g * slab : (g + 1) * slab], 0.0)
-            packed = piece if packed is None else packed + piece
-        back_send[s] = packed
+            part_j = jnp.dot(back_picks[j], piece, preferred_element_type=f32)
+            value = part_j if value is None else value + part_j
+        for i in range(per):
+            packed = None
+            for g in range(replicas):
+                at = i * CAPACITY + g * slab
+                piece = jnp.where(group == g, value[at : at + slab], 0.0)
+                packed = piece if packed is None else packed + piece
+            back_send[j * per + i] = packed
 
     def back_copy(n):
         s = lax.rem(n, domains)
@@ -307,6 +324,8 @@
         mean_copy(n).start()
     mean_land[0] = packed
 
+    lax.fori_loop(blocks // 2, blocks, convert, 0)
+
     def wait_back(n, carry):
         back_copy(n).wait_recv()
         return carry
@@ -319,24 +338,40 @@
             [turned(messages, g) for g in range(replicas)], axis=0
         )
     adj_e[...] = dot3(perm_b[...], ret[...].reshape(slots, LANES))
-    def finish(a):
-        turn = lax.rem(a, 2)
+    def ready(a, turn):
+        for k in range(listed):
+            b = lst[k, a]
+            scale = (energy_unit * norm) * cw_v[b] * adj_e[pl.ds(a * listed + k, 1), :]
+            rows = jnp.concatenate([scale, m_v[b] * scale], axis=0)
+            if k < listed - dense:
+                coefs[turn, k * 4 : k * 4 + 4, :] = rows
+            else:
+                at = k - listed + dense
+                stack = jnp.concatenate([*split(rows), jnp.zeros((4, LANES), f32)], axis=0)
+                left_s[turn, :, at * LANES : (at + 1) * LANES] = stack.astype(bf16)
+
+    def finish(a, turn):
         flat = [jnp.sum(jnp.transpose(sums[turn, c]), axis=0, keepdims=True) for c in range(4)]
+        both = dense_s[turn, :, 0:LANES] + dense_s[turn, :, LANES : 2 * LANES]
+        flat = [flat[c] + (both[c : c + 1] + both[c + 4 : c + 5] + both[c + 8 : c + 9]) for c in range(4)]
         here = pl.ds(pl.multiple_of(a * LANES, LANES), LANES)
         for c in range(3):
             f_ref[c, :, here] = x_v[c, :, here] * flat[0] - flat[c + 1]
 
-    def forces(a, carry):
-        turn = lax.rem(a, 2)
-        for k in range(listed):
-            b = lst[k, a]
-            scale = (energy_unit * norm) * cw_v[b] * adj_e[pl.ds(a * listed + k, 1), :]
-            coefs[k * 4 : k * 4 + 4, :] = jnp.concatenate([scale, m_v[b] * scale], axis=0)
+    def force_block(a, turn):
+        finish(lax.rem(a + blocks - 1, blocks), 1 - turn)
+        dense_total = jnp.zeros((16, 2 * LANES), f32)
         for h in range(0, LANES, STRIP):
+            share = dense * STRIP // LANES
+            if share:
+                here = slice(h // STRIP * share * LANES, (h // STRIP + 1) * share * LANES)
+                dense_total = dense_total + jnp.dot(
+                    left_s[turn, :, here], gt_v[a, here, :], preferred_element_type=f32
+                )
             acc = [[jnp.zeros((8, LANES), f32) for _ in range(STRIP // 8)] for _ in range(4)]
-            for k in range(listed):
+            for k in range(listed - dense):
                 rows = [
-                    jnp.broadcast_to(coefs[k * 4 + c : k * 4 + c + 1, :], (8, LANES)) for c in range(4)
+                    jnp.broadcast_to(coefs[turn, k * 4 + c : k * 4 + c + 1, :], (8, LANES)) for c in range(4)
                 ]
                 for q in range(STRIP // 8):
                     g = g_v[a * listed + k, h + q * 8 : h + q * 8 + 8, :]
@@ -345,12 +380,19 @@
             for c in range(4):
                 for q in range(STRIP // 8):
                     sums[turn, c, h + q * 8 : h + q * 8 + 8, :] = acc[c][q]
-        finish(lax.rem(a + blocks - 1, blocks))
-        return carry
-
-    sums[(blocks - 1) % 2] = jnp.zeros((4, LANES, LANES), f32)
-    lax.fori_loop(0, blocks, forces, 0)
-    finish(blocks - 1)
+        dense_s[turn] = dense_total
+        ready(lax.rem(a + 1, blocks), 1 - turn)
+
+    def forces(n, carry):
+        force_block(2 * n, 0)
+        force_block(2 * n + 1, 1)
+        return carry
+
+    ready(0, 0)
+    sums[1] = jnp.zeros((4, LANES, LANES), f32)
+    dense_s[1] = jnp.zeros((16, 2 * LANES), f32)
+    lax.fori_loop(0, blocks // 2, forces, 0)
+    finish(blocks - 1, 1)
     for n in range(1, replicas):
         mean_copy(n).wait_recv()
     messages = [mean_land[source[q]] for q in range(replicas)]
@@ -369,15 +411,9 @@
         mean_copy(n).wait_send()
 
 
-def hand_over(f_h, mean_h, f_out, mean_out, sems):
-    copies = [
-        pltpu.make_async_copy(f_h, f_out, sems.at[0]),
-        pltpu.make_async_copy(mean_h, mean_out, sems.at[1]),
-    ]
-    for copy in copies:
-        copy.start()
-    for copy in copies:
-        copy.wait()
+def hand_over(f_ref, mean_ref, f_out, mean_out):
+    f_out[...] = f_ref[...]
+    mean_out[...] = mean_ref[...]
 
 
 def shards(
@@ -394,6 +430,7 @@
     devices = domains * replicas
     slab = CAPACITY // replicas
     per = LANES // CAPACITY
+    dense = listed // 2 if slots == entries else listed // 4
     x = coords.transpose(1, 0, 2)
     cm = comp_means.reshape(3, comp_blocks, LANES).transpose(1, 0, 2)
     cv = comp_var.reshape(comp_blocks, 1, LANES)
@@ -402,7 +439,7 @@
     far = pl.BlockSpec(memory_space=pltpu.HBM)
     dma = pltpu.SemaphoreType.DMA
     forces, mean = pl.pallas_call(
-        functools.partial(step_kernel, replicas, domains, blocks, listed, owned),
+        functools.partial(step_kernel, replicas, domains, blocks, listed, owned, dense),
         in_specs=[far] * 11,
         out_specs=[whole] * 2,
         out_shape=[
@@ -427,7 +464,6 @@
             VMEM((2, listed // 2, 32, 2 * LANES), bf16),
             VMEM((entries, LANES), f32),
             VMEM((entries, LANES), i32),
-            VMEM((entries, LANES), i32),
             VMEM((slots, entries), bf16),
             VMEM((entries, slots), bf16),
             VMEM((slots // LANES, 8, LANES), f32),
@@ -441,7 +477,11 @@
             VMEM((owned // replicas, LANES), f32),
             VMEM((replicas, owned // replicas, LANES), f32),
             VMEM((2, 4, LANES, LANES), f32),
-            VMEM((4 * listed, LANES), f32),
+            VMEM((2, 4 * (listed - dense), LANES), f32),
+            VMEM((blocks, dense * LANES, 2 * LANES), bf16),
+            VMEM((2, 16, dense * LANES), bf16),
+            VMEM((2, 16, 2 * LANES), f32),
+            VMEM((domains // per, LANES, owned), bf16),
             dma((11,)),
             dma((domains,)),
             dma((domains,)),
@@ -453,7 +493,7 @@
             dma((replicas,)),
         ],
         compiler_params=pltpu.CompilerParams(
-            collective_id=0, has_side_effects=True, vmem_limit_bytes=60 << 20
+            collective_id=0, has_side_effects=True, vmem_limit_bytes=62 << 20
         ),
         name="step",
     )(
@@ -463,13 +503,12 @@
     )
     forces, mean = pl.pallas_call(
         hand_over,
-        in_specs=[far] * 2,
-        out_specs=[far] * 2,
+        in_specs=[whole] * 2,
+        out_specs=[whole] * 2,
         out_shape=[
             jax.ShapeDtypeStruct(x.shape, f32),
             jax.ShapeDtypeStruct((owned, LANES), f32),
         ],
-        scratch_shapes=[dma((2,))],
         name="hand_over",
     )(forces, mean)
     return (mean.reshape(-1), forces.transpose(1, 0, 2))

time: 63.7 us -> 51.5 us (0.81)
  Pallas kernels: 62.9 us -> 50.3 us
    pallas_call x1, Pallas kernels: 56.3 us -> 48.7 us  [shards(): pl.pallas_call(functools.partial(step_kernel, replicas, domains, blocks,...]
    pallas_call x1, Pallas kernels: 6.58 us -> 1.61 us  [shards(): pl.pallas_call(hand_over, in_specs=[whole] * 2, out_specs=[whole] * 2, ou...]
where the time goes in v3:
time: 51.5 us; the launch traced here: 51 us
  Pallas kernels  50.3 us (98%)
  between operations  0.64 us (1%)
    pallas_call x1, Pallas kernels, shards(): pl.pallas_call(functools.partial(step_kernel, replicas, domains, blocks,...  48.7 us
    pallas_call x1, Pallas kernels, shards(): pl.pallas_call(hand_over, in_specs=[whole] * 2, out_specs=[whole] * 2, ou...  1.61 us

profile of v3, /device:TPU:1, one launch (start us, length us, event | category | flops | bytes accessed | tf_op | source)
XLA Modules:
  0.0 51.0 jit_solution(14928802091081131235)
XLA Ops:
  0.6 48.7 %step.1 = (f32[3,1,4096]{2,1,0:T(1,128)}, f32[256,128]{1,0:T(8,128)}) custom-call(s32[32]{0:T(128)} %live_h.1, s32[16,32]{1,0:T(8,128)} %bitcast.21, s32[2048]{0:T(1024)} %owner_h.1, f32[3,1,4096]{2,1,0:T(1,128)} %bitcast.18, f32[32,128]{1,0:T(8,128)} %bitcast.19, f32[32,128]{1,0:T(8,128)} %bitcast.20, f32[2048,3,128]{2,1,0:T(4,128)} %bitcast.13, ...), custom_call_target="tpu_custom_call" | custom-call | tf_op jit(solution)/shard_map/step/pallas_call | solution.py:441
  49.4 1.6 %hand_over.1 = (f32[3,1,4096]{2,1,0:T(1,128)}, f32[256,128]{1,0:T(8,128)}) custom-call(f32[3,1,4096]{2,1,0:T(1,128)} %get-tuple-element.6.f_ref, f32[256,128]{1,0:T(8,128)} %get-tuple-element.7.mean_ref), custom_call_target="tpu_custom_call" | custom-call | tf_op jit(solution)/shard_map/hand_over/pallas_call | solution.py:504

commit v4 on v3

--- a/solution.py
+++ b/solution.py
@@ -33,9 +33,9 @@
     return [piece.astype(bf16) for piece in split(value)]
 
 
-def dot3(picks, value):
+def routed(picks, value):
     total = None
-    for piece in pieces_of(value):
+    for piece in pieces_of(value)[:2]:
         part = jnp.dot(picks, piece, preferred_element_type=f32)
         total = part if total is None else total + part
     return total
@@ -49,8 +49,8 @@
     replicas, domains, blocks, listed, owned, dense,
     live_h, lst_h, owner_h, x_h, av_h, aw_h, m_h, cv_h, cw_h, target_h, sigma_h,
     f_ref, mean_ref,
-    live, lst, owner, x_v, av_v, aw_v, m_v, cv_v, cw_v, target_v, sigma_v,
-    g_v, lhs_s, avt_s, rhs_s, part, place_s, perm_a, perm_b, slot_send, slot_land,
+    live, lst, owner, x_v, av_v, aw_v, table, target_v, sigma_v,
+    g_v, lhs_s, avt_s, sum_s, cws, rhs_s, part, place_s, perm_a, perm_b, slot_send, slot_land,
     out_send, out_land, back_send, back_land, ret, adj_e, mean_send, mean_land, sums, coefs, gt_v, left_s, dense_s, back_picks,
     loads, slot_ss, slot_rs, out_ss, out_rs, back_ss, back_rs, mean_ss, mean_rs,
 ):
@@ -67,7 +67,7 @@
         pltpu.make_async_copy(src, dst, loads.at[i])
         for i, (src, dst) in enumerate(
             [(lst_h, lst), (owner_h, owner), (live_h, live), (x_h, x_v), (av_h, av_v), (aw_h, aw_v),
-             (m_h, m_v), (cv_h, cv_v), (cw_h, cw_v), (target_h, target_v), (sigma_h, sigma_v)]
+             (m_h, table.at[:, 0:3, :]), (cv_h, table.at[:, 3:4, :]), (cw_h, table.at[:, 4:5, :]), (target_h, target_v), (sigma_h, sigma_v)]
         )
     ]
     for fetch in fetches:
@@ -126,6 +126,11 @@
     for fetch in fetches[6:]:
         fetch.wait()
     none = jnp.zeros((8, LANES), f32)
+    row8 = iota((8, LANES), 0)
+    fourth = jnp.where(row8 == 3, 1.0, 0.0)
+
+    def last(value):
+        return jnp.where(row8 == 7, jnp.broadcast_to(value, (8, LANES)), 0.0)
 
     def prepare(a, turn):
         x = jnp.concatenate(
@@ -134,42 +139,60 @@
         xx = jnp.sum(x * x, axis=0, keepdims=True)
         av = av_v[pl.ds(a, 1), :]
         lw = jnp.where(lane < live[a], jnp.log2(aw_v[pl.ds(a, 1), :]), dead)
-        left = jnp.concatenate(
-            [half_log2e * -2.0 * x, half_log2e * one, half_log2e * xx + av * lw, lw, zero, zero], axis=0
-        )
+        half = half_log2e * one
+        left = jnp.concatenate([half_log2e * -2.0 * x, lw, half, half, half, half * xx + av * lw], axis=0)
         l0, l1, l2 = split(left)
-        big = jnp.concatenate([l0, l0, l1, l1, l0, l2, none, none], axis=0)
-        lhs_s[turn] = jnp.transpose(big.astype(bf16))
+        a0, a1, a2 = split(av)
+        scaled_rows = jnp.concatenate([l0, l0, l1, l1, l0, l2, none, none], axis=0)
+        width_rows = jnp.concatenate(
+            [fourth + last(a0), fourth, last(a1), none, fourth, last(a2), none, none], axis=0
+        )
+        lhs_s[turn, 0:LANES] = jnp.transpose(scaled_rows.astype(bf16))
+        lhs_s[turn, LANES : 2 * LANES] = jnp.transpose(width_rows.astype(bf16))
         avt_s[turn] = jnp.transpose(jnp.broadcast_to(av, (LANES, LANES)))
         for k in range(listed):
-            b = lst[k, a]
-            m = m_v[b]
-            mm = jnp.sum(m * m, axis=0, keepdims=True)
-            r0, r1, r2 = split(jnp.concatenate([m, mm, one, cv_v[b], zero, zero], axis=0))
+            tile = table[lst[k, a]]
+            squares = pltpu.roll(tile * tile, 4, axis=0)
+            r0, r1, r2 = split(jnp.where(row8 < 4, tile, jnp.where(row8 == 7, 1.0, squares)))
             here = slice((k % 2) * LANES, (k % 2 + 1) * LANES)
             rhs_s[turn, k // 2, 0:16, here] = jnp.concatenate([r0, r1], axis=0).astype(bf16)
             rhs_s[turn, k // 2, 16:32, here] = jnp.concatenate([r2, r0], axis=0).astype(bf16)
 
+    def gather(a, turn):
+        for h in range(0, listed, 8):
+            total = sum_s[turn, pl.ds(h * 8, 8, stride=8), :]
+            for r in range(1, 8):
+                total = total + sum_s[turn, pl.ds(h * 8 + r, 8, stride=8), :]
+            part[pl.ds(pl.multiple_of(a * listed + h, 8), 8), :] = total * (norm * cws[turn, h : h + 8, :])
+
     blank = jnp.zeros((16, 2 * LANES), bf16)
 
     def pair_block(a, turn):
-        lhs = lhs_s[turn]
+        gather(lax.rem(a + blocks - 1, blocks), 1 - turn)
         for k in range(0, listed, 2):
             upper, lower = rhs_s[turn, k // 2, 0:16], rhs_s[turn, k // 2, 16:32]
             rhs = jnp.concatenate([upper, upper, lower, blank], axis=0)
+            both = k % 4 == 0
+            lhs = lhs_s[turn] if both else lhs_s[turn, 0:LANES]
             scaled = jnp.dot(lhs, rhs, preferred_element_type=f32)
             for i in range(2):
                 e = a * listed + k + i
                 b = lst[k + i, a]
-                cv = jnp.broadcast_to(cv_v[b], (8, LANES))
+                if not both:
+                    cv = jnp.broadcast_to(table[b, 3:4, :], (8, LANES))
                 total = jnp.zeros((8, LANES), f32)
+                here = slice(i * LANES, (i + 1) * LANES)
                 for h in range(0, LANES, 8):
-                    root = lax.rsqrt(avt_s[turn, h : h + 8, :] + cv)
+                    if both:
+                        root = lax.rsqrt(scaled[LANES + h : LANES + h + 8, here])
+                    else:
+                        root = lax.rsqrt(avt_s[turn, h : h + 8, :] + cv)
                     inv = root * root
-                    ov = (root * inv) * jnp.exp2(scaled[h : h + 8, i * LANES : (i + 1) * LANES] * inv)
+                    ov = (root * inv) * jnp.exp2(scaled[h : h + 8, here] * inv)
                     total = total + ov
                     g_v[e, h : h + 8, :] = ov * inv
-                part[pl.ds(e, 1), :] = jnp.sum(total, axis=0, keepdims=True) * (norm * cw_v[b])
+                sum_s[turn, (k + i) * 8 : (k + i) * 8 + 8, :] = total
+                cws[turn, k + i : k + i + 1, :] = table[b, 4:5, :]
         prepare(lax.rem(a + 1, blocks), 1 - turn)
 
     def pairs(n, carry):
@@ -177,6 +200,8 @@
         pair_block(2 * n + 1, 1)
         return carry
 
+    sum_s[1] = jnp.zeros((8 * listed, LANES), f32)
+    cws[1] = jnp.zeros((listed, LANES), f32)
     prepare(0, 0)
     early = blocks // 8
     lax.fori_loop(0, early, pairs, 0)
@@ -185,6 +210,7 @@
         slot_copy(s).start()
     slot_land[0] = slot_send[me_d // per]
     lax.fori_loop(early, blocks // 2, pairs, 0)
+    gather(blocks - 1, 1)
 
     def turned(pieces, to):
         total = None
@@ -202,7 +228,7 @@
             shift = 2 * shift
         return value
 
-    placed = dot3(perm_a[...], part[...]).reshape(domains, replicas, slab, LANES)
+    placed = routed(perm_a[...], part[...]).reshape(domains, replicas, slab, LANES)
     parts = [placed[:, g].reshape(domains * slab, LANES) for g in range(replicas)]
     for q in range(replicas):
         out_send[q] = turned(parts, q).reshape(domains, slab, LANES)
@@ -211,8 +237,15 @@
         to_r, to_d = peer(s)
         return pltpu.make_async_remote_copy(
             src_ref=out_send.at[to_r, to_d], dst_ref=out_land.at[s],
-            send_sem=out_ss.at[s], recv_sem=out_rs.at[s],
+            send_sem=out_ss, recv_sem=out_rs,
             device_id=(to_r, to_d), device_id_type=MESH,
+        )
+
+    def all_of(land, send_sem, recv_sem):
+        others = land.at[pl.ds(1, devices - 1)]
+        return pltpu.make_async_remote_copy(
+            src_ref=others, dst_ref=others, send_sem=send_sem, recv_sem=recv_sem,
+            device_id=peer(1), device_id_type=MESH,
         )
 
     def start_out(s, carry):
@@ -263,11 +296,7 @@
             ).astype(bf16)
     lax.fori_loop(0, blocks // 2, convert, 0)
 
-    def wait_out(s, carry):
-        out_copy(s).wait_recv()
-        return carry
-
-    lax.fori_loop(1, devices, wait_out, 0)
+    all_of(out_land, out_ss, out_rs).wait_recv()
     spread = []
     for s in range(domains):
         total = out_land[s]
@@ -275,10 +304,10 @@
             total = total + out_land[r * domains + s]
         for g in range(replicas):
             spread.append(jnp.where(group == g, total, 0.0))
-    mean = fold(dot3(picks, jnp.concatenate(spread, axis=0))) / replicas
+    mean = fold(routed(picks, jnp.concatenate(spread, axis=0))) / replicas
     misfit = mean - wanted
     adjoint = misfit / (sigmas * sigmas + 0.5 * misfit * misfit) / replicas
-    adjoints = pieces_of(adjoint)
+    adjoints = pieces_of(adjoint)[:2]
     for j in range(domains // per):
         value = None
         for piece in adjoints:
@@ -297,7 +326,7 @@
         to = lax.rem(me_r + n // domains, replicas), lax.rem(me_d + domains - s, domains)
         return pltpu.make_async_remote_copy(
             src_ref=back_send.at[s], dst_ref=back_land.at[n],
-            send_sem=back_ss.at[n], recv_sem=back_rs.at[n],
+            send_sem=back_ss, recv_sem=back_rs,
             device_id=to, device_id_type=MESH,
         )
 
@@ -326,23 +355,19 @@
 
     lax.fori_loop(blocks // 2, blocks, convert, 0)
 
-    def wait_back(n, carry):
-        back_copy(n).wait_recv()
-        return carry
-
-    lax.fori_loop(1, devices, wait_back, 0)
+    all_of(back_land, back_ss, back_rs).wait_recv()
     source = [lax.rem(me_r + replicas - q, replicas) for q in range(replicas)]
     for s in range(domains):
         messages = [back_land[source[q] * domains + s] for q in range(replicas)]
         ret[lax.rem(me_d + s, domains)] = jnp.concatenate(
             [turned(messages, g) for g in range(replicas)], axis=0
         )
-    adj_e[...] = dot3(perm_b[...], ret[...].reshape(slots, LANES))
+    adj_e[...] = routed(perm_b[...], ret[...].reshape(slots, LANES))
     def ready(a, turn):
         for k in range(listed):
-            b = lst[k, a]
-            scale = (energy_unit * norm) * cw_v[b] * adj_e[pl.ds(a * listed + k, 1), :]
-            rows = jnp.concatenate([scale, m_v[b] * scale], axis=0)
+            tile = table[lst[k, a]]
+            scale = (energy_unit * norm) * tile[4:5] * adj_e[pl.ds(a * listed + k, 1), :]
+            rows = (jnp.where(row8 == 3, 1.0, tile) * jnp.broadcast_to(scale, (8, LANES)))[0:4]
             if k < listed - dense:
                 coefs[turn, k * 4 : k * 4 + 4, :] = rows
             else:
@@ -356,7 +381,7 @@
         flat = [flat[c] + (both[c : c + 1] + both[c + 4 : c + 5] + both[c + 8 : c + 9]) for c in range(4)]
         here = pl.ds(pl.multiple_of(a * LANES, LANES), LANES)
         for c in range(3):
-            f_ref[c, :, here] = x_v[c, :, here] * flat[0] - flat[c + 1]
+            f_ref[c, :, here] = x_v[c, :, here] * flat[3] - flat[c]
 
     def force_block(a, turn):
         finish(lax.rem(a + blocks - 1, blocks), 1 - turn)
@@ -399,12 +424,8 @@
     for g in range(replicas):
         mean_ref[g * chunk : (g + 1) * chunk, :] = turned(messages, g)
 
-    def sent(s, carry):
-        out_copy(s).wait_send()
-        back_copy(s).wait_send()
-        return carry
-
-    lax.fori_loop(1, devices, sent, 0)
+    all_of(out_land, out_ss, out_rs).wait_send()
+    all_of(back_land, back_ss, back_rs).wait_send()
     for s in range(1, domains):
         slot_copy(s).wait_send()
     for n in range(1, replicas):
@@ -453,14 +474,14 @@
             VMEM(x.shape, f32),
             VMEM((blocks, LANES), f32),
             VMEM((blocks, LANES), f32),
-            VMEM(cm.shape, f32),
-            VMEM(cv.shape, f32),
-            VMEM(cw.shape, f32),
+            VMEM((comp_blocks, 8, LANES), f32),
             VMEM((owned, LANES), f32),
             VMEM((owned, LANES), f32),
             VMEM((entries, LANES, LANES), f32),
-            VMEM((2, LANES, ROWS), bf16),
+            VMEM((2, 2 * LANES, ROWS), bf16),
             VMEM((2, LANES, LANES), f32),
+            VMEM((2, 8 * listed, LANES), f32),
+            VMEM((2, listed, LANES), f32),
             VMEM((2, listed // 2, 32, 2 * LANES), bf16),
             VMEM((entries, LANES), f32),
             VMEM((entries, LANES), i32),
@@ -485,15 +506,15 @@
             dma((11,)),
             dma((domains,)),
             dma((domains,)),
-            dma((devices,)),
-            dma((devices,)),
-            dma((devices,)),
-            dma((devices,)),
+            dma,
+            dma,
+            dma,
+            dma,
             dma((replicas,)),
             dma((replicas,)),
         ],
         compiler_params=pltpu.CompilerParams(
-            collective_id=0, has_side_effects=True, vmem_limit_bytes=62 << 20
+            collective_id=0, has_side_effects=True, vmem_limit_bytes=63 << 20
         ),
         name="step",
     )(

time: 51.5 us -> 49 us (0.951)
  Pallas kernels: 50.3 us -> 47.8 us
    pallas_call x1, Pallas kernels: 48.7 us -> 46.2 us  [shards(): pl.pallas_call(functools.partial(step_kernel, replicas, domains, blocks,...]
where the time goes in v4:
time: 49 us; the launch traced here: 48.4 us
  Pallas kernels  47.8 us (98%)
  between operations  0.64 us (1%)
    pallas_call x1, Pallas kernels, shards(): pl.pallas_call(functools.partial(step_kernel, replicas, domains, blocks,...  46.2 us
    pallas_call x1, Pallas kernels, shards(): pl.pallas_call(hand_over, in_specs=[whole] * 2, out_specs=[whole] * 2, ou...  1.61 us

profile of v4, /device:TPU:1, one launch (start us, length us, event | category | flops | bytes accessed | tf_op | source)
XLA Modules:
  0.0 48.4 jit_solution(5256911328747211064)
XLA Ops:
  0.6 46.2 %step.1 = (f32[3,1,4096]{2,1,0:T(1,128)}, f32[256,128]{1,0:T(8,128)}) custom-call(s32[32]{0:T(128)} %live_h.1, s32[16,32]{1,0:T(8,128)} %bitcast.21, s32[2048]{0:T(1024)} %owner_h.1, f32[3,1,4096]{2,1,0:T(1,128)} %bitcast.18, f32[32,128]{1,0:T(8,128)} %bitcast.19, f32[32,128]{1,0:T(8,128)} %bitcast.20, f32[2048,3,128]{2,1,0:T(4,128)} %bitcast.13, ...), custom_call_target="tpu_custom_call" | custom-call | tf_op jit(solution)/shard_map/step/pallas_call | solution.py:462
  46.8 1.6 %hand_over.1 = (f32[3,1,4096]{2,1,0:T(1,128)}, f32[256,128]{1,0:T(8,128)}) custom-call(f32[3,1,4096]{2,1,0:T(1,128)} %get-tuple-element.6.f_ref, f32[256,128]{1,0:T(8,128)} %get-tuple-element.7.mean_ref), custom_call_target="tpu_custom_call" | custom-call | tf_op jit(solution)/shard_map/hand_over/pallas_call | solution.py:525

commit v5 on v4

--- a/solution.py
+++ b/solution.py
@@ -51,8 +51,8 @@
     f_ref, mean_ref,
     live, lst, owner, x_v, av_v, aw_v, table, target_v, sigma_v,
     g_v, lhs_s, avt_s, sum_s, cws, rhs_s, part, place_s, perm_a, perm_b, slot_send, slot_land,
-    out_send, out_land, back_send, back_land, ret, adj_e, mean_send, mean_land, sums, coefs, gt_v, left_s, dense_s, back_picks,
-    loads, slot_ss, slot_rs, out_ss, out_rs, back_ss, back_rs, mean_ss, mean_rs,
+    out_send, core_land, pair_send, out_land, back_send, back_land, ret, adj_e, mean_send, mean_land, sums, coefs, gt_v, left_s, dense_s, back_picks,
+    loads, slot_ss, slot_rs, core_ss, core_rs, out_ss, out_rs, back_ss, back_rs, swap_ss, swap_rs, mean_ss, mean_rs,
 ):
     me_r = lax.axis_index("rep")
     me_d = lax.axis_index("dom")
@@ -63,6 +63,9 @@
     per = LANES // CAPACITY
     devices = replicas * domains
     chunk = owned // replicas
+    chips = replicas // 2
+    cells = chips * domains
+    core = lax.rem(me_r, 2)
     fetches = [
         pltpu.make_async_copy(src, dst, loads.at[i])
         for i, (src, dst) in enumerate(
@@ -233,27 +236,45 @@
     for q in range(replicas):
         out_send[q] = turned(parts, q).reshape(domains, slab, LANES)
 
-    def out_copy(s):
-        to_r, to_d = peer(s)
+    partner = (me_r + 1 - 2 * core, me_d)
+
+    def core_copy(n):
         return pltpu.make_async_remote_copy(
-            src_ref=out_send.at[to_r, to_d], dst_ref=out_land.at[s],
+            src_ref=out_send.at[2 * n + 1 - core], dst_ref=core_land.at[n],
+            send_sem=core_ss.at[n], recv_sem=core_rs.at[n],
+            device_id=partner, device_id_type=MESH,
+        )
+
+    def pair_peer(n, sign):
+        to_r = lax.rem(me_r + 2 * (n // domains), replicas)
+        return to_r, lax.rem(me_d + domains + sign * lax.rem(n, domains), domains)
+
+    def out_copy(n):
+        to_r, to_d = pair_peer(n, 1)
+        return pltpu.make_async_remote_copy(
+            src_ref=pair_send.at[to_r // 2, to_d], dst_ref=out_land.at[n],
             send_sem=out_ss, recv_sem=out_rs,
             device_id=(to_r, to_d), device_id_type=MESH,
         )
 
     def all_of(land, send_sem, recv_sem):
-        others = land.at[pl.ds(1, devices - 1)]
+        others = land.at[pl.ds(1, cells - 1)]
         return pltpu.make_async_remote_copy(
             src_ref=others, dst_ref=others, send_sem=send_sem, recv_sem=recv_sem,
-            device_id=peer(1), device_id_type=MESH,
-        )
-
-    def start_out(s, carry):
-        out_copy(s).start()
-        return carry
-
-    lax.fori_loop(1, devices, start_out, 0)
-    out_land[0] = out_send[me_r, me_d]
+            device_id=partner, device_id_type=MESH,
+        )
+
+    def start_out(n, carry):
+        out_copy(n).start()
+        return carry
+
+    for n in range(chips):
+        core_copy(n).start()
+    for n in range(chips):
+        core_copy(n).wait_recv()
+        pair_send[n] = out_send[2 * n + core] + core_land[n]
+    lax.fori_loop(1, cells, start_out, 0)
+    out_land[0] = pair_send[me_r // 2, me_d]
 
     def convert(a, carry):
         for k in range(dense):
@@ -300,7 +321,7 @@
     spread = []
     for s in range(domains):
         total = out_land[s]
-        for r in range(1, replicas):
+        for r in range(1, chips):
             total = total + out_land[r * domains + s]
         for g in range(replicas):
             spread.append(jnp.where(group == g, total, 0.0))
@@ -322,20 +343,18 @@
             back_send[j * per + i] = packed
 
     def back_copy(n):
-        s = lax.rem(n, domains)
-        to = lax.rem(me_r + n // domains, replicas), lax.rem(me_d + domains - s, domains)
         return pltpu.make_async_remote_copy(
-            src_ref=back_send.at[s], dst_ref=back_land.at[n],
+            src_ref=back_send.at[lax.rem(n, domains)], dst_ref=back_land.at[0, n],
             send_sem=back_ss, recv_sem=back_rs,
-            device_id=to, device_id_type=MESH,
+            device_id=pair_peer(n, -1), device_id_type=MESH,
         )
 
     def start_back(n, carry):
         back_copy(n).start()
         return carry
 
-    lax.fori_loop(1, devices, start_back, 0)
-    back_land[0] = back_send[0]
+    lax.fori_loop(1, cells, start_back, 0)
+    back_land[0, 0] = back_send[0]
     packed = None
     for g in range(replicas):
         piece = jnp.where(group == g, mean[g * chunk : (g + 1) * chunk], 0.0)
@@ -355,10 +374,19 @@
 
     lax.fori_loop(blocks // 2, blocks, convert, 0)
 
-    all_of(back_land, back_ss, back_rs).wait_recv()
+    all_of(back_land.at[0], back_ss, back_rs).wait_recv()
+    swap = pltpu.make_async_remote_copy(
+        src_ref=back_land.at[0], dst_ref=back_land.at[1], send_sem=swap_ss, recv_sem=swap_rs,
+        device_id=partner, device_id_type=MESH,
+    )
+    swap.start()
+    swap.wait_recv()
     source = [lax.rem(me_r + replicas - q, replicas) for q in range(replicas)]
     for s in range(domains):
-        messages = [back_land[source[q] * domains + s] for q in range(replicas)]
+        messages = [
+            back_land[lax.rem(core + q, 2), lax.rem(me_r // 2 + chips - q // 2, chips) * domains + s]
+            for q in range(replicas)
+        ]
         ret[lax.rem(me_d + s, domains)] = jnp.concatenate(
             [turned(messages, g) for g in range(replicas)], axis=0
         )
@@ -425,7 +453,10 @@
         mean_ref[g * chunk : (g + 1) * chunk, :] = turned(messages, g)
 
     all_of(out_land, out_ss, out_rs).wait_send()
-    all_of(back_land, back_ss, back_rs).wait_send()
+    all_of(back_land.at[0], back_ss, back_rs).wait_send()
+    swap.wait_send()
+    for n in range(chips):
+        core_copy(n).wait_send()
     for s in range(1, domains):
         slot_copy(s).wait_send()
     for n in range(1, replicas):
@@ -448,7 +479,8 @@
     owned = target.shape[0] // LANES
     entries = blocks * listed
     slots = domains * CAPACITY
-    devices = domains * replicas
+    chips = replicas // 2
+    cells = chips * domains
     slab = CAPACITY // replicas
     per = LANES // CAPACITY
     dense = listed // 2 if slots == entries else listed // 4
@@ -490,9 +522,11 @@
             VMEM((slots // LANES, 8, LANES), f32),
             VMEM((domains, 8, LANES), f32),
             VMEM((replicas, domains, slab, LANES), f32),
-            VMEM((devices, slab, LANES), f32),
+            VMEM((chips, domains, slab, LANES), f32),
+            VMEM((chips, domains, slab, LANES), f32),
+            VMEM((cells, slab, LANES), f32),
             VMEM((domains, slab, LANES), f32),
-            VMEM((devices, slab, LANES), f32),
+            VMEM((2, cells, slab, LANES), f32),
             VMEM((domains, CAPACITY, LANES), f32),
             VMEM((entries, LANES), f32),
             VMEM((owned // replicas, LANES), f32),
@@ -506,6 +540,10 @@
             dma((11,)),
             dma((domains,)),
             dma((domains,)),
+            dma((chips,)),
+            dma((chips,)),
+            dma,
+            dma,
             dma,
             dma,
             dma,

time: 49 us -> 46.9 us (0.957)
  Pallas kernels: 47.8 us -> 46 us
    pallas_call x1, Pallas kernels: 46.2 us -> 44.4 us  [shards(): pl.pallas_call(functools.partial(step_kernel, replicas, domains, blocks,...]
where the time goes in v5:
time: 46.9 us; the launch traced here: 46.7 us
  Pallas kernels  46 us (98%)
  between operations  0.64 us (1%)
    pallas_call x1, Pallas kernels, shards(): pl.pallas_call(functools.partial(step_kernel, replicas, domains, blocks,...  44.4 us
    pallas_call x1, Pallas kernels, shards(): pl.pallas_call(hand_over, in_specs=[whole] * 2, out_specs=[whole] * 2, ou...  1.61 us

profile of v5, /device:TPU:1, one launch (start us, length us, event | category | flops | bytes accessed | tf_op | source)
XLA Modules:
  0.0 46.7 jit_solution(4508671625690693023)
XLA Ops:
  0.6 44.4 %step.1 = (f32[3,1,4096]{2,1,0:T(1,128)}, f32[256,128]{1,0:T(8,128)}) custom-call(s32[32]{0:T(128)} %live_h.1, s32[16,32]{1,0:T(8,128)} %bitcast.21, s32[2048]{0:T(1024)} %owner_h.1, f32[3,1,4096]{2,1,0:T(1,128)} %bitcast.18, f32[32,128]{1,0:T(8,128)} %bitcast.19, f32[32,128]{1,0:T(8,128)} %bitcast.20, f32[2048,3,128]{2,1,0:T(4,128)} %bitcast.13, ...), custom_call_target="tpu_custom_call" | custom-call | tf_op jit(solution)/shard_map/step/pallas_call | solution.py:494
  45.1 1.6 %hand_over.1 = (f32[3,1,4096]{2,1,0:T(1,128)}, f32[256,128]{1,0:T(8,128)}) custom-call(f32[3,1,4096]{2,1,0:T(1,128)} %get-tuple-element.6.f_ref, f32[256,128]{1,0:T(8,128)} %get-tuple-element.7.mean_ref), custom_call_target="tpu_custom_call" | custom-call | tf_op jit(solution)/shard_map/hand_over/pallas_call | solution.py:563

commit v6 on v5

--- a/solution.py
+++ b/solution.py
@@ -61,7 +61,6 @@
     width = LANES // replicas
     slab = CAPACITY // replicas
     per = LANES // CAPACITY
-    devices = replicas * domains
     chunk = owned // replicas
     chips = replicas // 2
     cells = chips * domains
@@ -77,14 +76,19 @@
         fetch.start()
     barrier = pltpu.get_barrier_semaphore()
 
-    def peer(s):
-        return lax.rem(me_r + s // domains, replicas), lax.rem(me_d + lax.rem(s, domains), domains)
-
-    def greet(s, carry):
-        pl.semaphore_signal(barrier, inc=1, device_id=peer(s), device_id_type=MESH)
-        return carry
-
-    lax.fori_loop(1, devices, greet, 0)
+    def pair_peer(n, sign):
+        to_r = lax.rem(me_r + 2 * (n // domains), replicas)
+        return to_r, lax.rem(me_d + domains + sign * lax.rem(n, domains), domains)
+
+    def greet(n, carry):
+        pl.semaphore_signal(barrier, inc=1, device_id=pair_peer(n, 1), device_id_type=MESH)
+        return carry
+
+    lax.fori_loop(1, cells, greet, 0)
+    for n in range(1, replicas, 2):
+        pl.semaphore_signal(
+            barrier, inc=1, device_id=(lax.rem(me_r + n, replicas), me_d), device_id_type=MESH
+        )
     for fetch in fetches[:6]:
         fetch.wait()
 
@@ -106,8 +110,7 @@
     rank = jnp.dot(before, hot.astype(bf16), preferred_element_type=f32)
     rank = jnp.sum(rank * hot, axis=1, keepdims=True)
     place = dev * CAPACITY + jnp.broadcast_to(rank, (entries, LANES)).astype(i32)
-    for j in range(slots // LANES):
-        perm_b[:, j * LANES : (j + 1) * LANES] = jnp.where(place == lane + j * LANES, 1.0, 0.0).astype(bf16)
+    place_s[...] = place
     place_f = place.astype(f32)
     for j in range(entries // LANES):
         row = jnp.transpose(place_f[j * LANES : (j + 1) * LANES])[0:1].astype(i32)
@@ -175,7 +178,7 @@
         for k in range(0, listed, 2):
             upper, lower = rhs_s[turn, k // 2, 0:16], rhs_s[turn, k // 2, 16:32]
             rhs = jnp.concatenate([upper, upper, lower, blank], axis=0)
-            both = k % 4 == 0
+            both = k % 8 == 0
             lhs = lhs_s[turn] if both else lhs_s[turn, 0:LANES]
             scaled = jnp.dot(lhs, rhs, preferred_element_type=f32)
             for i in range(2):
@@ -208,7 +211,7 @@
     prepare(0, 0)
     early = blocks // 8
     lax.fori_loop(0, early, pairs, 0)
-    pl.semaphore_wait(barrier, devices - 1)
+    pl.semaphore_wait(barrier, cells - 1 + chips)
     for s in range(1, domains):
         slot_copy(s).start()
     slot_land[0] = slot_send[me_d // per]
@@ -245,10 +248,6 @@
             device_id=partner, device_id_type=MESH,
         )
 
-    def pair_peer(n, sign):
-        to_r = lax.rem(me_r + 2 * (n // domains), replicas)
-        return to_r, lax.rem(me_d + domains + sign * lax.rem(n, domains), domains)
-
     def out_copy(n):
         to_r, to_d = pair_peer(n, 1)
         return pltpu.make_async_remote_copy(
@@ -265,7 +264,7 @@
         )
 
     def start_out(n, carry):
-        out_copy(n).start()
+        out_copy(cells - n).start()
         return carry
 
     for n in range(chips):
@@ -315,7 +314,8 @@
             back_picks[j, :, i * span : (i + 1) * span] = jnp.where(
                 column[:, :span] == iota((1, span), 1) + (i * span + 1), 1.0, 0.0
             ).astype(bf16)
-    lax.fori_loop(0, blocks // 2, convert, 0)
+    first_part = blocks // 2
+    lax.fori_loop(0, first_part, convert, 0)
 
     all_of(out_land, out_ss, out_rs).wait_recv()
     spread = []
@@ -350,7 +350,7 @@
         )
 
     def start_back(n, carry):
-        back_copy(n).start()
+        back_copy(cells - n).start()
         return carry
 
     lax.fori_loop(1, cells, start_back, 0)
@@ -372,7 +372,15 @@
         mean_copy(n).start()
     mean_land[0] = packed
 
-    lax.fori_loop(blocks // 2, blocks, convert, 0)
+    lax.fori_loop(first_part, blocks, convert, 0)
+    for j in range(slots // LANES):
+        perm_b[:, j * LANES : (j + 1) * LANES] = jnp.where(place_s[...] == lane + j * LANES, 1.0, 0.0).astype(bf16)
+
+    for n in range(1, replicas):
+        mean_copy(n).wait_recv()
+    messages = [mean_land[lax.rem(me_r + replicas - q, replicas)] for q in range(replicas)]
+    for g in range(replicas):
+        mean_ref[g * chunk : (g + 1) * chunk, :] = turned(messages, g)
 
     all_of(back_land.at[0], back_ss, back_rs).wait_recv()
     swap = pltpu.make_async_remote_copy(
@@ -381,7 +389,6 @@
     )
     swap.start()
     swap.wait_recv()
-    source = [lax.rem(me_r + replicas - q, replicas) for q in range(replicas)]
     for s in range(domains):
         messages = [
             back_land[lax.rem(core + q, 2), lax.rem(me_r // 2 + chips - q // 2, chips) * domains + s]
@@ -446,12 +453,6 @@
     dense_s[1] = jnp.zeros((16, 2 * LANES), f32)
     lax.fori_loop(0, blocks // 2, forces, 0)
     finish(blocks - 1, 1)
-    for n in range(1, replicas):
-        mean_copy(n).wait_recv()
-    messages = [mean_land[source[q]] for q in range(replicas)]
-    for g in range(replicas):
-        mean_ref[g * chunk : (g + 1) * chunk, :] = turned(messages, g)
-
     all_of(out_land, out_ss, out_rs).wait_send()
     all_of(back_land.at[0], back_ss, back_rs).wait_send()
     swap.wait_send()

time: 46.9 us -> 45.9 us (0.979)
  Pallas kernels: 46 us -> 44.8 us
    pallas_call x1, Pallas kernels: 44.4 us -> 43.2 us  [shards(): pl.pallas_call(functools.partial(step_kernel, replicas, domains, blocks,...]
where the time goes in v6:
time: 45.9 us; the launch traced here: 45.5 us
  Pallas kernels  44.8 us (98%)
  between operations  0.64 us (1%)
    pallas_call x1, Pallas kernels, shards(): pl.pallas_call(functools.partial(step_kernel, replicas, domains, blocks,...  43.2 us
    pallas_call x1, Pallas kernels, shards(): pl.pallas_call(hand_over, in_specs=[whole] * 2, out_specs=[whole] * 2, ou...  1.61 us

profile of v6, /device:TPU:1, one launch (start us, length us, event | category | flops | bytes accessed | tf_op | source)
XLA Modules:
  0.0 45.5 jit_solution(10600066667087420057)
XLA Ops:
  0.6 43.2 %step.1 = (f32[3,1,4096]{2,1,0:T(1,128)}, f32[256,128]{1,0:T(8,128)}) custom-call(s32[32]{0:T(128)} %live_h.1, s32[16,32]{1,0:T(8,128)} %bitcast.21, s32[2048]{0:T(1024)} %owner_h.1, f32[3,1,4096]{2,1,0:T(1,128)} %bitcast.18, f32[32,128]{1,0:T(8,128)} %bitcast.19, f32[32,128]{1,0:T(8,128)} %bitcast.20, f32[2048,3,128]{2,1,0:T(4,128)} %bitcast.13, ...), custom_call_target="tpu_custom_call" | custom-call | tf_op jit(solution)/shard_map/step/pallas_call | solution.py:495
  43.9 1.6 %hand_over.1 = (f32[3,1,4096]{2,1,0:T(1,128)}, f32[256,128]{1,0:T(8,128)}) custom-call(f32[3,1,4096]{2,1,0:T(1,128)} %get-tuple-element.6.f_ref, f32[256,128]{1,0:T(8,128)} %get-tuple-element.7.mean_ref), custom_call_target="tpu_custom_call" | custom-call | tf_op jit(solution)/shard_map/hand_over/pallas_call | solution.py:564
